TPU v7x, 32 devices: a whole 2x2x4 slice. The times are simulated.
32 devices in a mesh: ia: 4 (over y, x), ja: 2 (over core), ka: 4 (over z).
Axes of the slice: x: 2, y: 2, z: 4, core: 2. Of those that a mesh axis runs over, the one named last changes fastest.
Arguments:
- tensor: bfloat16 [128, 256, 1024], P('ia', 'ja', 'ka'), may hold values from 5 to 200
- factor_first: bfloat16 [128, 256], P('ia', ('ja', 'ka')), may hold values from 0.19921875 to 1.5
- factor_second: bfloat16 [256, 256], P('ja', ('ia', 'ka')), may hold values from 0.19921875 to 1.5
- factor_third: bfloat16 [1024, 256], P('ka', ('ia', 'ja')), may hold values from 0.19921875 to 1.5
Outputs:
- grad_first: float32 [128, 256], P('ia', ('ja', 'ka'))
- grad_second: float32 [256, 256], P('ja', ('ia', 'ka'))
- grad_third: float32 [1024, 256], P('ka', ('ia', 'ja'))
All inputs are finite; a program needn't handle non-finite values.
Results may differ from a plain program's by a relative error of at most 0.005.
Values may be sent and summed in bfloat16 or wider, within the bound.
No kernel may reach another device: no remote copies, remote signals or barrier semaphores. Data moves between devices by JAX's collectives and lax.ppermute only.
A program may use at most 64 MiB of HBM per device.

v0:
```python
import jax
import jax.numpy as jnp
from jax import lax
from jax.sharding import PartitionSpec as P


def body(tensor, factor_first, factor_second, factor_third):
    full_first = lax.all_gather(factor_first, ("ja", "ka"), axis=1, tiled=True)
    full_second = lax.all_gather(factor_second, ("ia", "ka"), axis=1, tiled=True)
    full_third = lax.all_gather(factor_third, ("ia", "ja"), axis=1, tiled=True)
    rows_i, rows_j, rows_k = tensor.shape
    rank = full_first.shape[1]
    total_i = rows_i * lax.axis_size("ia")
    total_j = rows_j * lax.axis_size("ja")
    total_k = rows_k * lax.axis_size("ka")
    first32 = full_first.astype(jnp.float32)
    second32 = full_second.astype(jnp.float32)
    khatri = (first32[:, None, :] * second32[None, :, :]).astype(jnp.bfloat16)
    khatri_flat = khatri.reshape(rows_i * rows_j, rank)
    model = jnp.einsum("mr,kr->mk", khatri_flat, full_third, preferred_element_type=jnp.float32)
    flat_data = tensor.reshape(rows_i * rows_j, rows_k).astype(jnp.float32)
    deriv = ((model - flat_data) * lax.rsqrt(model)).astype(jnp.bfloat16)
    part_third = jnp.einsum("mk,mr->kr", deriv, khatri_flat, preferred_element_type=jnp.float32)
    inner = jnp.einsum("mk,kr->mr", deriv, full_third, preferred_element_type=jnp.float32)
    inner = inner.reshape(rows_i, rows_j, rank)
    part_first = jnp.sum(inner * second32[None, :, :], axis=1) / (total_j * total_k)
    part_second = jnp.sum(inner * first32[:, None, :], axis=0) / (total_i * total_k)
    part_third = part_third / (total_i * total_j)
    grad_first = lax.psum_scatter(part_first, ("ja", "ka"), scatter_dimension=1, tiled=True)
    grad_second = lax.psum_scatter(part_second, ("ia", "ka"), scatter_dimension=1, tiled=True)
    grad_third = lax.psum_scatter(part_third, ("ia", "ja"), scatter_dimension=1, tiled=True)
    return (grad_first, grad_second, grad_third)


def solution(mesh):
    placed = (
        P("ia", "ja", "ka"),
        P("ia", ("ja", "ka")),
        P("ja", ("ia", "ka")),
        P("ka", ("ia", "ja")),
    )
    return jax.shard_map(
        body,
        mesh=mesh,
        in_specs=placed,
        out_specs=(P("ia", ("ja", "ka")), P("ja", ("ia", "ka")), P("ka", ("ia", "ja"))),
        check_vma=False,
    )
```

profile of v0, /device:TPU:0, one launch (start us, length us, event | category | flops | bytes accessed | tf_op | source)
XLA Modules:
  0.0 234.9 jit_solution(1074803909325882737)
XLA Ops:
  7.2 0.0 reduce-scatter.10.cloned.1.call-start
  7.2 0.8 copy.16
  8.0 25.6 %all_gather.9 = bf16[32,256]{0,1:T(8,128)(2,1)S(1)} all-gather(bf16[32,32]{0,1:T(8,128)(2,1)S(1)} %copy.16), channel_id=1, replica_groups=mesh['ia'=4,'ja'=2,'ka'=4] {'ja','ka'}, dimensions={1}, use_global_device_ids=true | all-gather | bytes 18432 | tf_op jit(solution)/shard_map/all_gather | solution.py:8
  33.6 0.1 copy.17
  33.7 41.3 %all_gather.10 = bf16[128,256]{0,1:T(8,128)(2,1)S(1)} all-gather(bf16[128,16]{0,1:T(8,128)(2,1)} %param.6), channel_id=1, replica_groups=mesh['ia'=4,'ja'=2,'ka'=4] {'ia','ka'}, dimensions={1}, use_global_device_ids=true | all-gather | bytes 69632 | tf_op jit(solution)/shard_map/all_gather | solution.py:9
  75.0 0.1 copy.18
  75.1 0.0 copy-start.1
  75.1 8.5 %all_gather.11 = bf16[256,256]{0,1:T(8,128)(2,1)S(1)} all-gather(bf16[256,32]{0,1:T(8,128)(2,1)} %param.7), channel_id=1, replica_groups=mesh['ia'=4,'ja'=2,'ka'=4] {'ia','ja'}, dimensions={1}, use_global_device_ids=true | all-gather | bytes 147456 | tf_op jit(solution)/shard_map/all_gather | solution.py:10
  83.6 0.6 multiply_convert_fusion
  84.3 0.0 copy-start
  84.3 0.0 copy-done.1
  84.3 0.9 fusion.1
  85.2 0.4 copy-done
  85.6 2.7 %multiply_reduce_fusion.1 = (f32[32,256]{1,0:T(8,128)S(1)}, f32[4096,256]{1,0:T(8,128)}) fusion(f32[128,256]{1,0:T(8,128)S(1)} %copy.18, bf16[4096,256]{1,0:T(8,128)(2,1)S(1)} %fusion.1, bf16[256,256]{0,1:T(8,128)(2,1)S(1)} %all_gather.11), kind=kOutput, calls=%fused_computation.4 | convolution fusion | flops 538959872 | bytes 6586368 | tf_op jit(solution)/shard_map/mk,kr->mr/dot_general | solution.py:24
  88.3 0.7 copy.20
  89.0 0.0 reduce-scatter.10.cloned.1.call-update
  89.0 0.0 reduce-scatter.12.cloned.1.call-start
  89.1 2.6 %multiply_reduce_fusion = f32[128,256]{1,0:T(8,128)S(1)} fusion(f32[32,128,256]{2,1,0:T(8,128)} %bitcast.16, f32[32,256]{1,0:T(8,128)S(1)} %convert_element_type.22), kind=kLoop, calls=%fused_computation.3 | loop fusion | flops 2064384 | bytes 4358144 | tf_op jit(solution)/shard_map/reduce_sum | solution.py:27
  91.7 0.8 copy.22
  92.4 0.0 reduce-scatter.12.cloned.1.call-update
  92.5 0.0 reduce-scatter.8.cloned.1.call-start
  92.5 3.2 %convolution_multiply_fusion = f32[256,256]{0,1:T(8,128)} fusion(bf16[4096,256]{1,0:T(8,128)(2,1)S(1)} %fusion.1, bf16[4096,256]{1,0:T(8,128)(2,1)} %bitcast.18), kind=kOutput, calls=%fused_computation.6 | convolution fusion | flops 536936448 | bytes 4456448 | tf_op jit(solution)/shard_map/mk,mr->kr/dot_general | solution.py:23
  95.7 0.0 reduce-scatter.8.cloned.1.call-update
  95.7 21.5 %reduce-scatter.10.cloned.1.call-done = f32[32,32]{1,0:T(8,128)} async-done(((f32[256,32]{1,0:T(8,128)}), f32[32,32]{1,0:T(8,128)}) %reduce-scatter.10.cloned.1.call-update) | async-done | bytes 4112
  117.3 1.4 copy.21
  118.7 75.9 %reduce-scatter.12.cloned.1.call-done = f32[16,128]{1,0:T(8,128)} async-done(((f32[256,128]{1,0:T(8,128)}), f32[16,128]{1,0:T(8,128)}) %reduce-scatter.12.cloned.1.call-update) | async-done | bytes 8208
  194.6 33.8 %reduce-scatter.8.cloned.1.call-done = f32[256,32]{0,1:T(8,128)} async-done(((f32[256,256]{0,1:T(8,128)}), f32[256,32]{0,1:T(8,128)}) %reduce-scatter.8.cloned.1.call-update) | async-done | bytes 32784 | tf_op jit(solution)/shard_map/reduce_scatter | solution.py:31
  (3 shorter events, 0.0 us)
Async XLA Ops:
  7.2 110.1 %reduce-scatter.10.cloned.1.call-start = ((), (), s32[]{:S(2)}) async-start(), calls=%async_computation.4 | async-start | bytes 147456
  75.1 9.2 %copy-start.1 = (bf16[32,128,256]{2,1,0:T(8,128)(2,1)S(1)}, bf16[32,128,256]{2,1,0:T(8,128)(2,1)}, u32[]{:S(2)}) copy-start(bf16[32,128,256]{2,1,0:T(8,128)(2,1)} %param.4) | copy-start | bytes 6291460
  84.3 1.3 copy-start
  89.0 105.6 %reduce-scatter.12.cloned.1.call-start = ((), (), s32[]{:S(2)}) async-start(), calls=%async_computation.5 | async-start | bytes 139264
  92.5 136.0 %reduce-scatter.8.cloned.1.call-start = ((), (), s32[]{:S(2)}) async-start(), calls=%async_computation.3 | async-start | bytes 294912 | tf_op jit(solution)/shard_map/reduce_scatter | solution.py:31
Sparse Core Ops, SparseCore 0:
  89.2 28.0 reduce-scatter.9
  120.2 74.3 reduce-scatter.11
  198.2 30.1 reduce-scatter.7
where the time goes:
time: 235 us
  waiting for transfers between devices  131 us (56%)
  blocking collectives  75.4 us (32%)
  between operations  13.8 us (6%)
  matrix products  6.78 us (3%)
  local copies, waits for them, and re-layouts  4.27 us (2%)
  other arithmetic  3.22 us (1%)
    unnamed x5, waiting for transfers between devices  97.5 us
    all_gather x1, blocking collectives, body(): lax.all_gather(factor_second, ('ia', 'ka'), axis=1, tiled=True)  41.3 us
    reduce_scatter x1, waiting for transfers between devices, body(): lax.psum_scatter(part_third, ('ia', 'ja'), scatter_dimension=1, tiled=True)  33.8 us
    all_gather x1, blocking collectives, body(): full_first = lax.all_gather(factor_first, ('ja', 'ka'), axis=1, tiled=True)  25.6 us
    all_gather x1, blocking collectives, body(): full_third = lax.all_gather(factor_third, ('ia', 'ja'), axis=1, tiled=True)  8.54 us
  transfers between devices with their start and end apart: 3, of which 3 were waited for; matrix products, arithmetic and copies ran while one was open for 3% of the time, Pallas kernels for 0%

commit v1 on v0

--- a/solution.py
+++ b/solution.py
@@ -4,15 +4,48 @@
 from jax.sharding import PartitionSpec as P
 
 
+def _a2a(x, axes):
+    n, m = x.shape
+    tile = 128 * (16 if x.dtype == jnp.bfloat16 else 8)
+    padded = -(-m // tile) * tile
+    if padded != m:
+        x = jnp.pad(x, ((0, 0), (0, padded - m)))
+    y = lax.all_to_all(x.reshape(n, padded // 128, 128), axes, 0, 0, tiled=True)
+    return y.reshape(n, padded)[:, :m]
+
+
+def _group_size(axes):
+    n = 1
+    for x in axes:
+        n *= lax.axis_size(x)
+    return n
+
+
+def gather_group(piece, axes):
+    n = _group_size(axes)
+    flat = piece.reshape(1, -1)
+    return _a2a(jnp.broadcast_to(flat, (n, flat.shape[1])), axes)
+
+
+def reduce_group(chunks, axes):
+    return jnp.sum(_a2a(chunks.reshape(chunks.shape[0], -1), axes), axis=0)
+
+
 def body(tensor, factor_first, factor_second, factor_third):
-    full_first = lax.all_gather(factor_first, ("ja", "ka"), axis=1, tiled=True)
-    full_second = lax.all_gather(factor_second, ("ia", "ka"), axis=1, tiled=True)
-    full_third = lax.all_gather(factor_third, ("ia", "ja"), axis=1, tiled=True)
+    nia, nja, nka = (lax.axis_size(a) for a in ("ia", "ja", "ka"))
     rows_i, rows_j, rows_k = tensor.shape
-    rank = full_first.shape[1]
-    total_i = rows_i * lax.axis_size("ia")
-    total_j = rows_j * lax.axis_size("ja")
-    total_k = rows_k * lax.axis_size("ka")
+    c1, c2, c3 = factor_first.shape[1], factor_second.shape[1], factor_third.shape[1]
+    rank = c1 * nja * nka
+    g1 = gather_group(factor_first, ("ja", "ka"))
+    full_first = g1.reshape(nja * nka, rows_i, c1).transpose(1, 0, 2).reshape(rows_i, rank)
+    g2 = gather_group(factor_second, ("ia", "ka"))
+    full_second = g2.reshape(nia * nka, rows_j, c2).transpose(1, 0, 2).reshape(rows_j, rank)
+    g3 = gather_group(factor_third, ("ia", "ja"))
+    full_third = g3.reshape(nia * nja, rows_k, c3).transpose(1, 0, 2).reshape(rows_k, rank)
+
+    total_i = rows_i * nia
+    total_j = rows_j * nja
+    total_k = rows_k * nka
     first32 = full_first.astype(jnp.float32)
     second32 = full_second.astype(jnp.float32)
     khatri = (first32[:, None, :] * second32[None, :, :]).astype(jnp.bfloat16)
@@ -26,9 +59,13 @@
     part_first = jnp.sum(inner * second32[None, :, :], axis=1) / (total_j * total_k)
     part_second = jnp.sum(inner * first32[:, None, :], axis=0) / (total_i * total_k)
     part_third = part_third / (total_i * total_j)
-    grad_first = lax.psum_scatter(part_first, ("ja", "ka"), scatter_dimension=1, tiled=True)
-    grad_second = lax.psum_scatter(part_second, ("ia", "ka"), scatter_dimension=1, tiled=True)
-    grad_third = lax.psum_scatter(part_third, ("ia", "ja"), scatter_dimension=1, tiled=True)
+
+    s1 = part_first.reshape(rows_i, nja * nka, c1).transpose(1, 0, 2)
+    s2 = part_second.reshape(rows_j, nia * nka, c2).transpose(1, 0, 2)
+    s3 = part_third.reshape(rows_k, nia * nja, c3).transpose(1, 0, 2)
+    grad_first = reduce_group(s1, ("ja", "ka")).reshape(rows_i, c1)
+    grad_second = reduce_group(s2, ("ia", "ka")).reshape(rows_j, c2)
+    grad_third = reduce_group(s3, ("ia", "ja")).reshape(rows_k, c3)
     return (grad_first, grad_second, grad_third)
 
 

time: 235 us -> 73.6 us (0.31)
  waiting for transfers between devices: 131 us -> 29.5 us
  blocking collectives: 75.4 us -> 0 us
  starting transfers between devices: 0.12 us -> 23.8 us
  between operations: 13.8 us -> 0.84 us
  local copies, waits for them, and re-layouts: 4.27 us -> 12.1 us
  other arithmetic: 3.22 us -> 0.71 us
    unnamed x5 -> x0, waiting for transfers between devices: 97.5 us -> none
    all_gather x3 -> x0, blocking collectives: 75.4 us -> none  [the longest x1 41.3 us: body(): lax.all_gather(factor_second, ('ia', 'ka'), axis=1, tiled=True)]
    reduce_scatter x1 -> x0, waiting for transfers between devices: 33.8 us -> none  [body(): lax.psum_scatter(part_third, ('ia', 'ja'), scatter_dimension=1, tiled=True)]
    all_to_all x0 -> x6, waiting for transfers between devices: none -> 29.5 us  [_a2a(): y = lax.all_to_all(x.reshape(n, padded // 128, 128), axes, 0, 0, tiled=True)]
    all_to_all x0 -> x6, starting transfers between devices: none -> 23.8 us  [_a2a(): y = lax.all_to_all(x.reshape(n, padded // 128, 128), axes, 0, 0, tiled=True)]
    another operation x0 -> x4, local copies, waits for them, and re-layouts: none -> 2.89 us  [the longest x3 2.65 us: _a2a(): y = lax.all_to_all(x.reshape(n, padded // 128, 128), axes, 0, 0, tiled=True)]
    reduce_sum x1 -> x3, other arithmetic: 2.56 us -> 0.05 us  [reduce_group(): return jnp.sum(_a2a(chunks.reshape(chunks.shape[0], -1), axes), axis=0)]
  transfers between devices with their start and end apart: 3 -> 6, of which waited for: 3 -> 6; matrix products, arithmetic and copies ran while one was open for 3% -> 13% of each run, Pallas kernels for 0% -> 0%
where the time goes in v1:
time: 73.6 us; the launch traced here: 72.8 us
  waiting for transfers between devices  29.5 us (40%)
  starting transfers between devices  23.8 us (32%)
  local copies, waits for them, and re-layouts  12.1 us (16%)
  matrix products  5.82 us (8%)
  between operations  0.84 us (1%)
    all_to_all x6, waiting for transfers between devices, _a2a(): y = lax.all_to_all(x.reshape(n, padded // 128, 128), axes, 0, 0, tiled=True)  29.5 us
    all_to_all x6, starting transfers between devices, _a2a(): y = lax.all_to_all(x.reshape(n, padded // 128, 128), axes, 0, 0, tiled=True)  23.8 us
    unnamed x7, local copies, waits for them, and re-layouts  3.43 us
    another operation x3, local copies, waits for them, and re-layouts, _a2a(): y = lax.all_to_all(x.reshape(n, padded // 128, 128), axes, 0, 0, tiled=True)  2.65 us
    dot_general x1, matrix products, body(): jnp.einsum('mk,mr->kr', deriv, khatri_flat, preferred_element_type=jnp.fl...  2.52 us
    dot_general x1, matrix products, body(): jnp.einsum('mr,kr->mk', khatri_flat, full_third, preferred_element_type=j...  2.38 us
    broadcast_in_dim x5, local copies, waits for them, and re-layouts, gather_group(): return _a2a(jnp.broadcast_to(flat, (n, flat.shape[1])), axes)  2.26 us
  transfers between devices with their start and end apart: 6, of which 6 were waited for; matrix products, arithmetic and copies ran while one was open for 13% of the time, Pallas kernels for 0%

profile of v1, /device:TPU:0, one launch (start us, length us, event | category | flops | bytes accessed | tf_op | source)
XLA Modules:
  0.0 72.8 jit_solution(499665597269543973)
XLA Ops:
  0.6 0.8 %broadcast_in_dim.10 = bf16[1024]{0:T(1024)(128)(2,1)S(1)} reshape(bf16[32,32]{1,0:T(8,128)(2,1)} %param.5) | data formatting | bytes 4096 | tf_op jit(solution)/shard_map/broadcast_in_dim | solution.py:27
  1.4 0.6 pad.10
  2.0 6.3 %all-to-all-start = ((bf16[8,16,128]{2,1,0:T(8,128)(2,1)}), bf16[8,16,128]{2,1,0:T(8,128)(2,1)S(1)}, u32[]{:S(2)}, u32[]{:S(2)}) async-start(bf16[8,16,128]{2,1,0:T(8,128)(2,1)} %pad.10), calls=%async_computation | async-start | bytes 65536 | tf_op jit(solution)/shard_map/all_to_all | solution.py:13
  8.4 0.8 %copy.33 = bf16[256,32]{1,0:T(8,128)(2,1)S(1)} copy(bf16[256,32]{0,1:T(8,128)(2,1)} %param.7) | data formatting | bytes 32768 | tf_op args[3]
  9.3 4.8 %all-to-all-done = bf16[8,16,128]{2,1,0:T(8,128)(2,1)S(1)} async-done(((bf16[8,16,128]{2,1,0:T(8,128)(2,1)}), bf16[8,16,128]{2,1,0:T(8,128)(2,1)S(1)}, u32[]{:S(2)}, u32[]{:S(2)}) %all-to-all-start) | async-done | bytes 32800 | tf_op jit(solution)/shard_map/all_to_all | solution.py:13
  14.2 0.7 broadcast_in_dim.27
  14.8 3.7 %all-to-all-start.2 = ((bf16[8,64,128]{2,1,0:T(8,128)(2,1)}), bf16[8,64,128]{2,1,0:T(8,128)(2,1)S(1)}, u32[]{:S(2)}, u32[]{:S(2)}) async-start(bf16[8,64,128]{2,1,0:T(8,128)(2,1)} %broadcast_in_dim.27), calls=%async_computation.2 | async-start | bytes 262144 | tf_op jit(solution)/shard_map/all_to_all | solution.py:13
  18.5 0.8 %copy.30 = bf16[128,16]{1,0:T(8,128)(2,1)S(1)} copy(bf16[128,16]{0,1:T(8,128)(2,1)} %param.6) | data formatting | bytes 8192 | tf_op args[2]
  19.4 4.6 %all-to-all-done.2 = bf16[8,64,128]{2,1,0:T(8,128)(2,1)S(1)} async-done(((bf16[8,64,128]{2,1,0:T(8,128)(2,1)}), bf16[8,64,128]{2,1,0:T(8,128)(2,1)S(1)}, u32[]{:S(2)}, u32[]{:S(2)}) %all-to-all-start.2) | async-done | bytes 131104 | tf_op jit(solution)/shard_map/all_to_all | solution.py:13
  24.1 0.6 broadcast_in_dim.12
  24.7 3.5 %all-to-all-start.1 = ((bf16[16,16,128]{2,1,0:T(8,128)(2,1)}), bf16[16,16,128]{2,1,0:T(8,128)(2,1)S(1)}, u32[]{:S(2)}, u32[]{:S(2)}) async-start(bf16[16,16,128]{2,1,0:T(8,128)(2,1)} %broadcast_in_dim.12), calls=%async_computation.1 | async-start | bytes 131072 | tf_op jit(solution)/shard_map/all_to_all | solution.py:13
  28.9 6.7 %all-to-all-done.1 = bf16[16,16,128]{2,1,0:T(8,128)(2,1)S(1)} async-done(((bf16[16,16,128]{2,1,0:T(8,128)(2,1)}), bf16[16,16,128]{2,1,0:T(8,128)(2,1)S(1)}, u32[]{:S(2)}, u32[]{:S(2)}) %all-to-all-start.1) | async-done | bytes 65568 | tf_op jit(solution)/shard_map/all_to_all | solution.py:13
  35.9 0.3 copy.31
  36.3 0.6 multiply_convert_fusion
  37.0 2.4 %fusion.1 = bf16[4096,256]{1,0:T(8,128)(2,1)S(1)} fusion(bf16[32,128,256]{2,1,0:T(8,128)(2,1)} %param.4, bf16[4096,256]{1,0:T(8,128)(2,1)S(1)} %bitcast.33, bf16[256,256]{0,1:T(8,128)(2,1)S(1)} %bitcast.40), kind=kOutput, calls=%fused_computation.2 | convolution fusion | flops 541065216 | bytes 6422528 | tf_op jit(solution)/shard_map/mr,kr->mk/dot_general | solution.py:53
  39.4 0.9 %multiply_reduce_fusion = (f32[128,256]{1,0:T(8,128)S(1)}, f32[32,256]{1,0:T(8,128)S(1)}) fusion(f32[32,256]{1,0:T(8,128)S(1)} %reshape.111, f32[128,256]{1,0:T(8,128)S(1)} %copy.32, bf16[32,128,256]{2,1,0:T(8,128)(2,1)S(1)} %bitcast.44, bf16[256,256,1]{0,1,2:T(8,128)(2,1)S(1)} %bitcast.41), kind=kOutput, calls=%fused_computation.3 | convolution fusion | flops 541024256 | bytes 2555904 | tf_op jit(solution)/shard_map/mk,kr->mr/dot_general | solution.py:57
  40.3 0.4 copy-done
  40.8 0.7 reshape_reshape.14
  41.5 3.3 %all-to-all-start.3 = ((f32[8,8,128]{2,1,0:T(8,128)}), f32[8,8,128]{2,1,0:T(8,128)S(1)}, u32[]{:S(2)}, u32[]{:S(2)}) async-start(f32[8,8,128]{2,1,0:T(8,128)} %reshape_reshape.14), calls=%async_computation.3 | async-start | bytes 65536 | tf_op jit(solution)/shard_map/all_to_all | solution.py:13
  44.9 2.5 %convolution_multiply_fusion = f32[256,256]{0,1:T(8,128)S(1)} fusion(bf16[4096,256]{1,0:T(8,128)(2,1)} %copy-done, bf16[4096,256]{1,0:T(8,128)(2,1)S(1)} %bitcast.34), kind=kOutput, calls=%fused_computation.6 | convolution fusion | flops 536936448 | bytes 4456448 | tf_op jit(solution)/shard_map/mk,mr->kr/dot_general | solution.py:56
  47.4 0.3 copy.39
  47.8 1.0 %reshape_reshape.16 = f32[8,64,128]{2,1,0:T(8,128)} reshape(f32[8,256,32]{2,1,0:T(8,128)S(1)} %bitcast.30) | data formatting | bytes 524288 | tf_op jit(solution)/shard_map/reshape;reshape | solution.py:13
  48.7 1.9 %all-to-all-done.3 = f32[8,8,128]{2,1,0:T(8,128)S(1)} async-done(((f32[8,8,128]{2,1,0:T(8,128)}), f32[8,8,128]{2,1,0:T(8,128)S(1)}, u32[]{:S(2)}, u32[]{:S(2)}) %all-to-all-start.3) | async-done | bytes 32800 | tf_op jit(solution)/shard_map/all_to_all | solution.py:13
  50.6 3.4 %all-to-all-start.5 = ((f32[8,64,128]{2,1,0:T(8,128)}), f32[8,64,128]{2,1,0:T(8,128)S(1)}, u32[]{:S(2)}, u32[]{:S(2)}) async-start(f32[8,64,128]{2,1,0:T(8,128)} %reshape_reshape.16), calls=%async_computation.5 | async-start | bytes 524288 | tf_op jit(solution)/shard_map/all_to_all | solution.py:13
  54.1 0.3 copy.38
  54.5 1.0 %reshape_reshape.15 = f32[16,16,128]{2,1,0:T(8,128)} reshape(f32[16,128,16]{2,1,0:T(8,128)S(1)} %copy.38) | data formatting | bytes 262144 | tf_op jit(solution)/shard_map/reshape;reshape | solution.py:13
  55.4 5.4 %all-to-all-done.5 = f32[8,64,128]{2,1,0:T(8,128)S(1)} async-done(((f32[8,64,128]{2,1,0:T(8,128)}), f32[8,64,128]{2,1,0:T(8,128)S(1)}, u32[]{:S(2)}, u32[]{:S(2)}) %all-to-all-start.5) | async-done | bytes 262176 | tf_op jit(solution)/shard_map/all_to_all | solution.py:13
  60.9 3.5 %all-to-all-start.4 = ((f32[16,16,128]{2,1,0:T(8,128)}), f32[16,16,128]{2,1,0:T(8,128)S(1)}, u32[]{:S(2)}, u32[]{:S(2)}) async-start(f32[16,16,128]{2,1,0:T(8,128)} %reshape_reshape.15), calls=%async_computation.4 | async-start | bytes 262144 | tf_op jit(solution)/shard_map/all_to_all | solution.py:13
  64.4 0.7 reshape.107
  65.2 0.7 copy.41
  65.9 6.1 %all-to-all-done.4 = f32[16,16,128]{2,1,0:T(8,128)S(1)} async-done(((f32[16,16,128]{2,1,0:T(8,128)}), f32[16,16,128]{2,1,0:T(8,128)S(1)}, u32[]{:S(2)}, u32[]{:S(2)}) %all-to-all-start.4) | async-done | bytes 131104 | tf_op jit(solution)/shard_map/all_to_all | solution.py:13
  72.1 0.7 copy.40
  (23 shorter events, 1.7 us)
Async XLA Ops:
  2.0 12.1 %all-to-all-start = ((bf16[8,16,128]{2,1,0:T(8,128)(2,1)}), bf16[8,16,128]{2,1,0:T(8,128)(2,1)S(1)}, u32[]{:S(2)}, u32[]{:S(2)}) async-start(bf16[8,16,128]{2,1,0:T(8,128)(2,1)} %pad.10), calls=%async_computation | async-start | bytes 65536 | tf_op jit(solution)/shard_map/all_to_all | solution.py:13
  14.8 9.3 %all-to-all-start.2 = ((bf16[8,64,128]{2,1,0:T(8,128)(2,1)}), bf16[8,64,128]{2,1,0:T(8,128)(2,1)S(1)}, u32[]{:S(2)}, u32[]{:S(2)}) async-start(bf16[8,64,128]{2,1,0:T(8,128)(2,1)} %broadcast_in_dim.27), calls=%async_computation.2 | async-start | bytes 262144 | tf_op jit(solution)/shard_map/all_to_all | solution.py:13
  24.7 10.9 %all-to-all-start.1 = ((bf16[16,16,128]{2,1,0:T(8,128)(2,1)}), bf16[16,16,128]{2,1,0:T(8,128)(2,1)S(1)}, u32[]{:S(2)}, u32[]{:S(2)}) async-start(bf16[16,16,128]{2,1,0:T(8,128)(2,1)} %broadcast_in_dim.12), calls=%async_computation.1 | async-start | bytes 131072 | tf_op jit(solution)/shard_map/all_to_all | solution.py:13
  39.4 1.4 %copy-start = (bf16[4096,256]{1,0:T(8,128)(2,1)}, bf16[4096,256]{1,0:T(8,128)(2,1)S(1)}, u32[]{:S(2)}) copy-start(bf16[4096,256]{1,0:T(8,128)(2,1)S(1)} %fusion.1) | copy-start | bytes 6291460
  41.5 9.0 %all-to-all-start.3 = ((f32[8,8,128]{2,1,0:T(8,128)}), f32[8,8,128]{2,1,0:T(8,128)S(1)}, u32[]{:S(2)}, u32[]{:S(2)}) async-start(f32[8,8,128]{2,1,0:T(8,128)} %reshape_reshape.14), calls=%async_computation.3 | async-start | bytes 65536 | tf_op jit(solution)/shard_map/all_to_all | solution.py:13
  50.6 10.3 %all-to-all-start.5 = ((f32[8,64,128]{2,1,0:T(8,128)}), f32[8,64,128]{2,1,0:T(8,128)S(1)}, u32[]{:S(2)}, u32[]{:S(2)}) async-start(f32[8,64,128]{2,1,0:T(8,128)} %reshape_reshape.16), calls=%async_computation.5 | async-start | bytes 524288 | tf_op jit(solution)/shard_map/all_to_all | solution.py:13
  60.9 11.1 %all-to-all-start.4 = ((f32[16,16,128]{2,1,0:T(8,128)}), f32[16,16,128]{2,1,0:T(8,128)S(1)}, u32[]{:S(2)}, u32[]{:S(2)}) async-start(f32[16,16,128]{2,1,0:T(8,128)} %reshape_reshape.15), calls=%async_computation.4 | async-start | bytes 262144 | tf_op jit(solution)/shard_map/all_to_all | solution.py:13

commit v2 on v0

--- a/solution.py
+++ b/solution.py
@@ -3,16 +3,78 @@
 from jax import lax
 from jax.sharding import PartitionSpec as P
 
+GROUPS = (("ja", "ka"), ("ia", "ka"), ("ia", "ja"))
+
+
+def _bits(n):
+    k = n.bit_length() - 1
+    assert 1 << k == n
+    return k
+
+
+def _bit(axis, t):
+    return (lax.axis_index(axis) // (1 << t)) % 2
+
+
+def _swap(x, axis, t):
+    n = lax.axis_size(axis)
+    return lax.ppermute(x, axis, [(i, i ^ (1 << t)) for i in range(n)])
+
+
+def _exchange(items, axis, t):
+    flat = [x.reshape(-1) for x in items]
+    sizes = [f.shape[0] for f in flat]
+    got = _swap(jnp.concatenate(flat) if len(flat) > 1 else flat[0], axis, t)
+    out, off = [], 0
+    for x, m in zip(items, sizes):
+        out.append(got[off:off + m].reshape(x.shape))
+        off += m
+    return out
+
+
+def gather_all(pieces):
+    accs = [p[None] for p in pieces]
+    for axis in ("ka", "ja", "ia"):
+        for t in range(_bits(lax.axis_size(axis))):
+            who = [f for f, g in enumerate(GROUPS) if axis in g]
+            got = _exchange([accs[f] for f in who], axis, t)
+            hi = _bit(axis, t) == 1
+            for f, r in zip(who, got):
+                accs[f] = jnp.where(hi, jnp.concatenate([r, accs[f]]), jnp.concatenate([accs[f], r]))
+    return accs
+
+
+def reduce_all(parts):
+    accs = list(parts)
+    for axis in ("ia", "ja", "ka"):
+        for t in reversed(range(_bits(lax.axis_size(axis)))):
+            who = [f for f, g in enumerate(GROUPS) if axis in g]
+            hi = _bit(axis, t) == 1
+            keep, send = [], []
+            for f in who:
+                m = accs[f].shape[0] // 2
+                lo_half, hi_half = accs[f][:m], accs[f][m:]
+                keep.append(jnp.where(hi, hi_half, lo_half))
+                send.append(jnp.where(hi, lo_half, hi_half))
+            got = _exchange(send, axis, t)
+            for f, k, r in zip(who, keep, got):
+                accs[f] = k + r
+    return [a[0] for a in accs]
+
 
 def body(tensor, factor_first, factor_second, factor_third):
-    full_first = lax.all_gather(factor_first, ("ja", "ka"), axis=1, tiled=True)
-    full_second = lax.all_gather(factor_second, ("ia", "ka"), axis=1, tiled=True)
-    full_third = lax.all_gather(factor_third, ("ia", "ja"), axis=1, tiled=True)
+    nia, nja, nka = (lax.axis_size(a) for a in ("ia", "ja", "ka"))
     rows_i, rows_j, rows_k = tensor.shape
-    rank = full_first.shape[1]
-    total_i = rows_i * lax.axis_size("ia")
-    total_j = rows_j * lax.axis_size("ja")
-    total_k = rows_k * lax.axis_size("ka")
+    c1, c2, c3 = factor_first.shape[1], factor_second.shape[1], factor_third.shape[1]
+    rank = c1 * nja * nka
+    g1, g2, g3 = gather_all([factor_first, factor_second, factor_third])
+    full_first = g1.transpose(1, 0, 2).reshape(rows_i, rank)
+    full_second = g2.transpose(1, 0, 2).reshape(rows_j, rank)
+    full_third = g3.transpose(1, 0, 2).reshape(rows_k, rank)
+
+    total_i = rows_i * nia
+    total_j = rows_j * nja
+    total_k = rows_k * nka
     first32 = full_first.astype(jnp.float32)
     second32 = full_second.astype(jnp.float32)
     khatri = (first32[:, None, :] * second32[None, :, :]).astype(jnp.bfloat16)
@@ -26,9 +88,11 @@
     part_first = jnp.sum(inner * second32[None, :, :], axis=1) / (total_j * total_k)
     part_second = jnp.sum(inner * first32[:, None, :], axis=0) / (total_i * total_k)
     part_third = part_third / (total_i * total_j)
-    grad_first = lax.psum_scatter(part_first, ("ja", "ka"), scatter_dimension=1, tiled=True)
-    grad_second = lax.psum_scatter(part_second, ("ia", "ka"), scatter_dimension=1, tiled=True)
-    grad_third = lax.psum_scatter(part_third, ("ia", "ja"), scatter_dimension=1, tiled=True)
+
+    s1 = part_first.reshape(rows_i, nja * nka, c1).transpose(1, 0, 2)
+    s2 = part_second.reshape(rows_j, nia * nka, c2).transpose(1, 0, 2)
+    s3 = part_third.reshape(rows_k, nia * nja, c3).transpose(1, 0, 2)
+    grad_first, grad_second, grad_third = reduce_all([s1, s2, s3])
     return (grad_first, grad_second, grad_third)
 
 

time: 235 us -> 57.2 us (0.24)
  waiting for transfers between devices: 131 us -> 17.9 us
  blocking collectives: 75.4 us -> 0 us
  starting transfers between devices: 0.12 us -> 18.8 us
  between operations: 13.8 us -> 1.26 us
  local copies, waits for them, and re-layouts: 4.27 us -> 10.7 us
  matrix products: 6.78 us -> 2.75 us
    unnamed x5 -> x0, waiting for transfers between devices: 97.5 us -> none
    all_gather x3 -> x0, blocking collectives: 75.4 us -> none  [the longest x1 41.3 us: body(): lax.all_gather(factor_second, ('ia', 'ka'), axis=1, tiled=True)]
    reduce_scatter x1 -> x0, waiting for transfers between devices: 33.8 us -> none  [body(): lax.psum_scatter(part_third, ('ia', 'ja'), scatter_dimension=1, tiled=True)]
    ppermute x0 -> x10, starting transfers between devices: none -> 18.8 us  [_swap(): return lax.ppermute(x, axis, [(i, i ^ 1 << t) for i in range(n)])]
    ppermute x0 -> x10, waiting for transfers between devices: none -> 17.9 us  [_swap(): return lax.ppermute(x, axis, [(i, i ^ 1 << t) for i in range(n)])]
    select_n x0 -> x18, other arithmetic: none -> 2.7 us  [the longest x8 2.47 us: gather_all(): jnp.where(hi, jnp.concatenate([r, accs[f]]), jnp.concatenate([accs[f], r]))]
    reduce_sum x1 -> x0, other arithmetic: 2.56 us -> none  [body(): jnp.sum(inner * first32[:, None, :], axis=0) / (total_i * total_k)]
    reshape x0 -> x24, local copies, waits for them, and re-layouts: none -> 2.42 us  [the longest x10 1.09 us: _exchange(): flat = [x.reshape(-1) for x in items]]
  transfers between devices with their start and end apart: 3 -> 10, of which waited for: 3 -> 10; matrix products, arithmetic and copies ran while one was open for 3% -> 5% of each run, Pallas kernels for 0% -> 0%
where the time goes in v2:
time: 57.2 us; the launch traced here: 56.5 us
  starting transfers between devices  18.8 us (33%)
  waiting for transfers between devices  17.9 us (31%)
  local copies, waits for them, and re-layouts  10.7 us (19%)
  other arithmetic  5 us (9%)
  matrix products  2.75 us (5%)
  between operations  1.26 us (2%)
    ppermute x10, starting transfers between devices, _swap(): return lax.ppermute(x, axis, [(i, i ^ 1 << t) for i in range(n)])  18.8 us
    ppermute x10, waiting for transfers between devices, _swap(): return lax.ppermute(x, axis, [(i, i ^ 1 << t) for i in range(n)])  17.9 us
    unnamed x5, local copies, waits for them, and re-layouts  2.5 us
    select_n x8, other arithmetic, gather_all(): jnp.where(hi, jnp.concatenate([r, accs[f]]), jnp.concatenate([accs[f], r]))  2.47 us
    slice x38, local copies, waits for them, and re-layouts, _exchange(): out.append(got[off:off + m].reshape(x.shape))  2.22 us
    select_n x12, local copies, waits for them, and re-layouts, gather_all(): jnp.where(hi, jnp.concatenate([r, accs[f]]), jnp.concatenate([accs[f], r]))  1.63 us
  transfers between devices with their start and end apart: 10, of which 10 were waited for; matrix products, arithmetic and copies ran while one was open for 5% of the time, Pallas kernels for 0%

profile of v2, /device:TPU:0, one launch (start us, length us, event | category | flops | bytes accessed | tf_op | source)
XLA Modules:
  0.0 56.5 jit_solution(12640894131214217394)
XLA Ops:
  0.6 0.8 %reshape_broadcast_in_dim.9 = bf16[1024]{0:T(1024)(128)(2,1)S(1)} reshape(bf16[32,32]{1,0:T(8,128)(2,1)} %param.5) | data formatting | bytes 4096 | tf_op jit(solution)/shard_map/reshape;broadcast_in_dim | solution.py:25
  1.4 0.8 %copy.40 = bf16[128,16]{1,0:T(8,128)(2,1)S(1)} copy(bf16[128,16]{0,1:T(8,128)(2,1)} %param.6) | data formatting | bytes 8192 | tf_op args[2]
  2.3 3.1 %collective-permute-start = (bf16[3072]{0:T(1024)(128)(2,1)S(1)}, bf16[3072]{0:T(1024)(128)(2,1)S(1)}, u32[]{:S(2)}, u32[]{:S(2)}) collective-permute-start(bf16[3072]{0:T(1024)(128)(2,1)S(1)} %pad_maximum_fusion.9), channel_id=1, source_target_pairs={{0,1},{1,0},{2,3},{3,2},{4,5},{5,4},{6,7},{7,6},{8,9},{9,8},{10,11... | collective-permute-start | bytes 18440 | tf_op jit(solution)/shard_map/ppermute | solution.py:21
  5.4 1.6 %collective-permute-done = bf16[3072]{0:T(1024)(128)(2,1)S(1)} collective-permute-done((bf16[3072]{0:T(1024)(128)(2,1)S(1)}, bf16[3072]{0:T(1024)(128)(2,1)S(1)}, u32[]{:S(2)}, u32[]{:S(2)}) %collective-permute-start) | collective-permute-done | bytes 6176 | tf_op jit(solution)/shard_map/ppermute | solution.py:21
  7.1 0.8 %maximum_select_fusion.7 = bf16[2,32,32]{2,1,0:T(8,128)(2,1)S(1)} fusion(bf16[1,32,32]{2,1,0:T(8,128)(2,1)} %bitcast.48, bf16[1,32,32]{2,1,0:T(8,128)(2,1)S(1)} %reshape.289, pred[]{:T(512)S(6)} %eq.31), kind=kLoop, calls=%fused_computation.42 | loop fusion | flops 6144 | bytes 8193 | tf_op jit(solution)/shard_map/jit(_where)/select_n | solution.py:43
  8.1 0.8 %maximum_select_fusion.9 = bf16[2,128,16]{1,2,0:T(8,128)(2,1)S(1)} fusion(bf16[1,128,16]{1,2,0:T(8,128)(2,1)} %bitcast.49, bf16[1,128,16]{1,2,0:T(8,128)(2,1)S(1)} %copy.41, pred[]{:T(512)S(6)} %eq.31), kind=kLoop, calls=%fused_computation.49 | loop fusion | flops 12288 | bytes 16385 | tf_op jit(solution)/shard_map/jit(_where)/select_n | solution.py:43
  9.2 3.1 %collective-permute-start.1 = (bf16[6144]{0:T(1024)(128)(2,1)S(1)}, bf16[6144]{0:T(1024)(128)(2,1)S(1)}, u32[]{:S(2)}, u32[]{:S(2)}) collective-permute-start(bf16[6144]{0:T(1024)(128)(2,1)S(1)} %pad_maximum_fusion.7), channel_id=1, source_target_pairs={{0,2},{1,3},{2,0},{3,1},{4,6},{5,7},{6,4},{7,5},{8,10},{9,11},{10,... | collective-permute-start | bytes 36872 | tf_op jit(solution)/shard_map/ppermute | solution.py:21
  12.3 0.8 %copy.44 = bf16[256,32]{1,0:T(8,128)(2,1)S(1)} copy(bf16[256,32]{0,1:T(8,128)(2,1)} %param.7) | data formatting | bytes 32768 | tf_op args[3]
  13.2 0.7 %collective-permute-done.1 = bf16[6144]{0:T(1024)(128)(2,1)S(1)} collective-permute-done((bf16[6144]{0:T(1024)(128)(2,1)S(1)}, bf16[6144]{0:T(1024)(128)(2,1)S(1)}, u32[]{:S(2)}, u32[]{:S(2)}) %collective-permute-start.1) | collective-permute-done | bytes 12320 | tf_op jit(solution)/shard_map/ppermute | solution.py:21
  14.7 0.9 %collective-permute-done.2 = bf16[12288]{0:T(1024)(128)(2,1)S(1)} collective-permute-done((bf16[12288]{0:T(1024)(128)(2,1)S(1)}, bf16[12288]{0:T(1024)(128)(2,1)S(1)}, u32[]{:S(2)}, u32[]{:S(2)}) %collective-permute-start.2) | collective-permute-done | bytes 24608 | tf_op jit(solution)/shard_map/ppermute | solution.py:21
  15.7 0.8 %maximum_select_fusion.5 = bf16[2,256,32]{1,2,0:T(8,128)(2,1)S(1)} fusion(bf16[1,256,32]{1,2,0:T(8,128)(2,1)} %bitcast.47, bf16[1,256,32]{1,2,0:T(8,128)(2,1)S(1)} %copy.49, pred[]{:T(512)S(6)} %eq.33), kind=kLoop, calls=%fused_computation.30 | loop fusion | flops 49152 | bytes 65537 | tf_op jit(solution)/shard_map/jit(_where)/select_n | solution.py:43
  16.8 1.9 %collective-permute-start.3 = (bf16[24576]{0:T(1024)(128)(2,1)S(1)}, bf16[24576]{0:T(1024)(128)(2,1)S(1)}, u32[]{:S(2)}, u32[]{:S(2)}) collective-permute-start(bf16[24576]{0:T(1024)(128)(2,1)S(1)} %pad_maximum_fusion.3), channel_id=1, source_target_pairs={{0,8},{8,0},{16,24},{24,16},{1,9},{9,1},{17,25},{25,17},{2,10},{10... | collective-permute-start | bytes 147464 | tf_op jit(solution)/shard_map/ppermute | solution.py:21
  18.8 2.2 %collective-permute-done.3 = bf16[24576]{0:T(1024)(128)(2,1)S(1)} collective-permute-done((bf16[24576]{0:T(1024)(128)(2,1)S(1)}, bf16[24576]{0:T(1024)(128)(2,1)S(1)}, u32[]{:S(2)}, u32[]{:S(2)}) %collective-permute-start.3) | collective-permute-done | bytes 49184 | tf_op jit(solution)/shard_map/ppermute | solution.py:21
  22.2 1.9 %collective-permute-start.4 = (bf16[49152]{0:T(1024)(128)(2,1)S(1)}, bf16[49152]{0:T(1024)(128)(2,1)S(1)}, u32[]{:S(2)}, u32[]{:S(2)}) collective-permute-start(bf16[49152]{0:T(1024)(128)(2,1)S(1)} %pad_maximum_fusion.1), channel_id=1, source_target_pairs={{0,16},{8,24},{16,0},{24,8},{1,17},{9,25},{17,1},{25,9},{2,18},{10... | collective-permute-start | bytes 294920 | tf_op jit(solution)/shard_map/ppermute | solution.py:21
  24.3 2.6 %collective-permute-done.4 = bf16[49152]{0:T(1024)(128)(2,1)S(1)} collective-permute-done((bf16[49152]{0:T(1024)(128)(2,1)S(1)}, bf16[49152]{0:T(1024)(128)(2,1)S(1)}, u32[]{:S(2)}, u32[]{:S(2)}) %collective-permute-start.4) | collective-permute-done | bytes 98336 | tf_op jit(solution)/shard_map/ppermute | solution.py:21
  27.7 0.6 %multiply_convert_fusion = bf16[32,128,256]{2,1,0:T(8,128)(2,1)S(1)} fusion(f32[128,256]{1,0:T(8,128)S(1)} %copy.60, f32[32,256]{1,0:T(8,128)S(1)} %reshape.311), kind=kLoop, calls=%fused_computation.5 | loop fusion | flops 2097152 | bytes 2260992 | tf_op jit(solution)/shard_map/convert_element_type | solution.py:80
  28.5 0.9 %fusion.1 = bf16[4096,256]{1,0:T(8,128)(2,1)S(1)} fusion(bf16[32,128,256]{2,1,0:T(8,128)(2,1)S(1)} %copy-done, bf16[4096,256]{1,0:T(8,128)(2,1)S(1)} %bitcast.37, bf16[256,256]{0,1:T(8,128)(2,1)S(1)} %bitcast.45), kind=kOutput, calls=%fused_computation.2 | convolution fusion | flops 541065216 | bytes 6422528 | tf_op jit(solution)/shard_map/mr,kr->mk/dot_general | solution.py:82
  29.4 1.0 %convolution_multiply_fusion = f32[256,256]{0,1:T(8,128)S(1)} fusion(bf16[4096,256]{1,0:T(8,128)(2,1)S(1)} %fusion.1, bf16[4096,256]{1,0:T(8,128)(2,1)S(1)} %bitcast.38), kind=kOutput, calls=%fused_computation.6 | convolution fusion | flops 536936448 | bytes 4456448 | tf_op jit(solution)/shard_map/mk,mr->kr/dot_general | solution.py:85
  30.3 0.9 %multiply_reduce_fusion.1 = (f32[32,256]{1,0:T(8,128)S(1)}, f32[128,256]{1,0:T(8,128)S(1)}) fusion(f32[128,256]{1,0:T(8,128)S(1)} %copy.60, f32[32,256]{1,0:T(8,128)S(1)} %reshape.311, bf16[32,128,256]{2,1,0:T(8,128)(2,1)S(1)} %bitcast.51, bf16[256,256,1]{0,1,2:T(8,128)(2,1)S(1)} %bitcast.46), kind=kOutput, calls=%fused_computation.4 | convolution fusion | flops 541024256 | bytes 2555904 | tf_op jit(solution)/shard_map/mk,kr->mr/dot_general | solution.py:86
  31.8 0.3 copy.65
  32.4 1.9 %collective-permute-start.5 = (f32[49152]{0:T(1024)S(1)}, f32[49152]{0:T(1024)S(1)}, u32[]{:S(2)}, u32[]{:S(2)}) collective-permute-start(f32[49152]{0:T(1024)S(1)} %pad_maximum_fusion), channel_id=1, source_target_pairs={{0,16},{8,24},{16,0},{24,8},{1,17},{9,25},{17,1},{25,9},{2,18},{10... | collective-permute-start | bytes 589832 | tf_op jit(solution)/shard_map/ppermute | solution.py:21
  34.4 3.7 %collective-permute-done.5 = f32[49152]{0:T(1024)S(1)} collective-permute-done((f32[49152]{0:T(1024)S(1)}, f32[49152]{0:T(1024)S(1)}, u32[]{:S(2)}, u32[]{:S(2)}) %collective-permute-start.5) | collective-permute-done | bytes 196640 | tf_op jit(solution)/shard_map/ppermute | solution.py:21
  39.3 1.9 %collective-permute-start.6 = (f32[24576]{0:T(1024)S(1)}, f32[24576]{0:T(1024)S(1)}, u32[]{:S(2)}, u32[]{:S(2)}) collective-permute-start(f32[24576]{0:T(1024)S(1)} %pad_maximum_fusion.2), channel_id=1, source_target_pairs={{0,8},{8,0},{16,24},{24,16},{1,9},{9,1},{17,25},{25,17},{2,10},{10... | collective-permute-start | bytes 294920 | tf_op jit(solution)/shard_map/ppermute | solution.py:21
  41.3 2.7 %collective-permute-done.6 = f32[24576]{0:T(1024)S(1)} collective-permute-done((f32[24576]{0:T(1024)S(1)}, f32[24576]{0:T(1024)S(1)}, u32[]{:S(2)}, u32[]{:S(2)}) %collective-permute-start.6) | collective-permute-done | bytes 98336 | tf_op jit(solution)/shard_map/ppermute | solution.py:21
  44.8 0.7 %collective-permute-done.7 = f32[12288]{0:T(1024)S(1)} collective-permute-done((f32[12288]{0:T(1024)S(1)}, f32[12288]{0:T(1024)S(1)}, u32[]{:S(2)}, u32[]{:S(2)}) %collective-permute-start.7) | collective-permute-done | bytes 49184 | tf_op jit(solution)/shard_map/ppermute | solution.py:21
  45.8 2.9 %collective-permute-start.8 = (f32[6144]{0:T(1024)S(1)}, f32[6144]{0:T(1024)S(1)}, u32[]{:S(2)}, u32[]{:S(2)}) collective-permute-start(f32[6144]{0:T(1024)S(1)} %pad_maximum_fusion.6), channel_id=1, source_target_pairs={{0,2},{1,3},{2,0},{3,1},{4,6},{5,7},{6,4},{7,5},{8,10},{9,11},{10,... | collective-permute-start | bytes 73736 | tf_op jit(solution)/shard_map/ppermute | solution.py:21
  48.8 1.7 %collective-permute-done.8 = f32[6144]{0:T(1024)S(1)} collective-permute-done((f32[6144]{0:T(1024)S(1)}, f32[6144]{0:T(1024)S(1)}, u32[]{:S(2)}, u32[]{:S(2)}) %collective-permute-start.8) | collective-permute-done | bytes 24608 | tf_op jit(solution)/shard_map/ppermute | solution.py:21
  51.2 2.0 %collective-permute-start.9 = (f32[3072]{0:T(1024)S(1)}, f32[3072]{0:T(1024)S(1)}, u32[]{:S(2)}, u32[]{:S(2)}) collective-permute-start(f32[3072]{0:T(1024)S(1)} %pad_maximum_fusion.8), channel_id=1, source_target_pairs={{0,1},{1,0},{2,3},{3,2},{4,5},{5,4},{6,7},{7,6},{8,9},{9,8},{10,11... | collective-permute-start | bytes 36872 | tf_op jit(solution)/shard_map/ppermute | solution.py:21
  53.2 0.7 %copy.78 = f32[256,32]{0,1:T(8,128)} copy(f32[256,32]{1,0:T(8,128)S(1)} %add_bitcast_fusion) | data formatting | bytes 65536
  53.9 1.1 %collective-permute-done.9 = f32[3072]{0:T(1024)S(1)} collective-permute-done((f32[3072]{0:T(1024)S(1)}, f32[3072]{0:T(1024)S(1)}, u32[]{:S(2)}, u32[]{:S(2)}) %collective-permute-start.9) | collective-permute-done | bytes 12320 | tf_op jit(solution)/shard_map/ppermute | solution.py:21
  55.1 0.6 %fusion.3 = f32[1,32,32]{2,0,1:T(1,128)} fusion(f32[1,32,32]{2,0,1:T(1,128)S(1)} %reshape.308, pred[]{:T(512)S(6)} %eq.31, f32[2,32,32]{2,0,1:T(2,128)S(1)} %copy_add_fusion.1), kind=kLoop, calls=%fused_computation.40 | loop fusion | flops 2048 | bytes 16385 | tf_op jit(solution)/shard_map/add | solution.py:61
  55.8 0.6 %add_bitcast_fusion.1 = f32[128,16]{0,1:T(8,128)} fusion(f32[1,128,16]{1,2,0:T(8,128)S(1)} %copy.77, f32[2,128,16]{1,2,0:T(8,128)S(1)} %select_add_fusion.4, pred[]{:T(512)S(6)} %eq.31), kind=kLoop, calls=%fused_computation.50 | loop fusion | flops 4096 | bytes 32769 | tf_op jit(solution)/shard_map/squeeze | solution.py:62
  (127 shorter events, 8.1 us)
Async XLA Ops:
  2.3 4.7 %collective-permute-start = (bf16[3072]{0:T(1024)(128)(2,1)S(1)}, bf16[3072]{0:T(1024)(128)(2,1)S(1)}, u32[]{:S(2)}, u32[]{:S(2)}) collective-permute-start(bf16[3072]{0:T(1024)(128)(2,1)S(1)} %pad_maximum_fusion.9), channel_id=1, source_target_pairs={{0,1},{1,0},{2,3},{3,2},{4,5},{5,4},{6,7},{7,6},{8,9},{9,8},{10,11... | collective-permute-start | bytes 18440 | tf_op jit(solution)/shard_map/ppermute | solution.py:21
  9.2 4.8 %collective-permute-start.1 = (bf16[6144]{0:T(1024)(128)(2,1)S(1)}, bf16[6144]{0:T(1024)(128)(2,1)S(1)}, u32[]{:S(2)}, u32[]{:S(2)}) collective-permute-start(bf16[6144]{0:T(1024)(128)(2,1)S(1)} %pad_maximum_fusion.7), channel_id=1, source_target_pairs={{0,2},{1,3},{2,0},{3,1},{4,6},{5,7},{6,4},{7,5},{8,10},{9,11},{10,... | collective-permute-start | bytes 36872 | tf_op jit(solution)/shard_map/ppermute | solution.py:21
  14.3 1.2 %collective-permute-start.2 = (bf16[12288]{0:T(1024)(128)(2,1)S(1)}, bf16[12288]{0:T(1024)(128)(2,1)S(1)}, u32[]{:S(2)}, u32[]{:S(2)}) collective-permute-start(bf16[12288]{0:T(1024)(128)(2,1)S(1)} %pad_maximum_fusion.5), channel_id=1, source_target_pairs={{0,4},{4,0},{1,5},{5,1},{2,6},{6,2},{3,7},{7,3},{8,12},{12,8},{9,1... | collective-permute-start | bytes 73736 | tf_op jit(solution)/shard_map/ppermute | solution.py:21
  16.8 4.2 %collective-permute-start.3 = (bf16[24576]{0:T(1024)(128)(2,1)S(1)}, bf16[24576]{0:T(1024)(128)(2,1)S(1)}, u32[]{:S(2)}, u32[]{:S(2)}) collective-permute-start(bf16[24576]{0:T(1024)(128)(2,1)S(1)} %pad_maximum_fusion.3), channel_id=1, source_target_pairs={{0,8},{8,0},{16,24},{24,16},{1,9},{9,1},{17,25},{25,17},{2,10},{10... | collective-permute-start | bytes 147464 | tf_op jit(solution)/shard_map/ppermute | solution.py:21
  22.2 4.7 %collective-permute-start.4 = (bf16[49152]{0:T(1024)(128)(2,1)S(1)}, bf16[49152]{0:T(1024)(128)(2,1)S(1)}, u32[]{:S(2)}, u32[]{:S(2)}) collective-permute-start(bf16[49152]{0:T(1024)(128)(2,1)S(1)} %pad_maximum_fusion.1), channel_id=1, source_target_pairs={{0,16},{8,24},{16,0},{24,8},{1,17},{9,25},{17,1},{25,9},{2,18},{10... | collective-permute-start | bytes 294920 | tf_op jit(solution)/shard_map/ppermute | solution.py:21
  26.9 1.6 %copy-start = (bf16[32,128,256]{2,1,0:T(8,128)(2,1)S(1)}, bf16[32,128,256]{2,1,0:T(8,128)(2,1)}, u32[]{:S(2)}) copy-start(bf16[32,128,256]{2,1,0:T(8,128)(2,1)} %param.4) | copy-start | bytes 6291460
  32.4 5.7 %collective-permute-start.5 = (f32[49152]{0:T(1024)S(1)}, f32[49152]{0:T(1024)S(1)}, u32[]{:S(2)}, u32[]{:S(2)}) collective-permute-start(f32[49152]{0:T(1024)S(1)} %pad_maximum_fusion), channel_id=1, source_target_pairs={{0,16},{8,24},{16,0},{24,8},{1,17},{9,25},{17,1},{25,9},{2,18},{10... | collective-permute-start | bytes 589832 | tf_op jit(solution)/shard_map/ppermute | solution.py:21
  39.3 4.7 %collective-permute-start.6 = (f32[24576]{0:T(1024)S(1)}, f32[24576]{0:T(1024)S(1)}, u32[]{:S(2)}, u32[]{:S(2)}) collective-permute-start(f32[24576]{0:T(1024)S(1)} %pad_maximum_fusion.2), channel_id=1, source_target_pairs={{0,8},{8,0},{16,24},{24,16},{1,9},{9,1},{17,25},{25,17},{2,10},{10... | collective-permute-start | bytes 294920 | tf_op jit(solution)/shard_map/ppermute | solution.py:21
  44.3 1.3 %collective-permute-start.7 = (f32[12288]{0:T(1024)S(1)}, f32[12288]{0:T(1024)S(1)}, u32[]{:S(2)}, u32[]{:S(2)}) collective-permute-start(f32[12288]{0:T(1024)S(1)} %pad_maximum_fusion.4), channel_id=1, source_target_pairs={{0,4},{4,0},{1,5},{5,1},{2,6},{6,2},{3,7},{7,3},{8,12},{12,8},{9,1... | collective-permute-start | bytes 147464 | tf_op jit(solution)/shard_map/ppermute | solution.py:21
  45.8 4.7 %collective-permute-start.8 = (f32[6144]{0:T(1024)S(1)}, f32[6144]{0:T(1024)S(1)}, u32[]{:S(2)}, u32[]{:S(2)}) collective-permute-start(f32[6144]{0:T(1024)S(1)} %pad_maximum_fusion.6), channel_id=1, source_target_pairs={{0,2},{1,3},{2,0},{3,1},{4,6},{5,7},{6,4},{7,5},{8,10},{9,11},{10,... | collective-permute-start | bytes 73736 | tf_op jit(solution)/shard_map/ppermute | solution.py:21
  51.2 3.8 %collective-permute-start.9 = (f32[3072]{0:T(1024)S(1)}, f32[3072]{0:T(1024)S(1)}, u32[]{:S(2)}, u32[]{:S(2)}) collective-permute-start(f32[3072]{0:T(1024)S(1)} %pad_maximum_fusion.8), channel_id=1, source_target_pairs={{0,1},{1,0},{2,3},{3,2},{4,5},{5,4},{6,7},{7,6},{8,9},{9,8},{10,11... | collective-permute-start | bytes 36872 | tf_op jit(solution)/shard_map/ppermute | solution.py:21

commit v3 on v2

v3 whole, which is shorter than its diff:
```python
import jax
import jax.numpy as jnp
from jax import lax
from jax.sharding import PartitionSpec as P

GROUPS = (("ja", "ka"), ("ia", "ka"), ("ia", "ja"))


def _digits(n):
    k = n.bit_length() - 1
    assert 1 << k == n
    out, t = [], 0
    while t < k:
        w = 2 if k - t >= 2 else 1
        out.append((t, 1 << w))
        t += w
    return out


def _digit(axis, t, r):
    return (lax.axis_index(axis) // (1 << t)) % r


def _exchange(items, axis, t, s):
    n = lax.axis_size(axis)
    flat = [x.reshape(-1) for x in items]
    sizes = [f.shape[0] for f in flat]
    payload = jnp.concatenate(flat) if len(flat) > 1 else flat[0]
    got = lax.ppermute(payload, axis, [(i, i ^ (s << t)) for i in range(n)])
    out, off = [], 0
    for x, m in zip(items, sizes):
        out.append(got[off:off + m].reshape(x.shape))
        off += m
    return out


def _flip_by(x, d, r):
    w = r.bit_length() - 1
    rest = x.shape[1:]
    y = x.reshape((2,) * w + rest)
    for p in range(w):
        y = jnp.where((d // (1 << p)) % 2 == 1, jnp.flip(y, w - 1 - p), y)
    return y.reshape((r,) + rest)


def _dense(x):
    flat = x.reshape(-1)
    lanes = 128 if flat.shape[0] % 128 == 0 else flat.shape[0]
    return flat.reshape(1, flat.shape[0] // lanes, lanes)


def gather_all(pieces):
    accs = [_dense(p) for p in pieces]
    for axis in ("ka", "ja", "ia"):
        for t, r in _digits(lax.axis_size(axis)):
            who = [f for f, g in enumerate(GROUPS) if axis in g]
            mine = [accs[f] for f in who]
            got = [_exchange(mine, axis, t, s) for s in range(1, r)]
            d = _digit(axis, t, r)
            for i, f in enumerate(who):
                cands = _flip_by(jnp.stack([mine[i]] + [g[i] for g in got]), d, r)
                accs[f] = cands.reshape((-1,) + cands.shape[2:])
    return accs


def reduce_all(parts):
    accs = list(parts)
    for axis in ("ia", "ja", "ka"):
        for t, r in reversed(_digits(lax.axis_size(axis))):
            who = [f for f, g in enumerate(GROUPS) if axis in g]
            d = _digit(axis, t, r)
            subs = [_flip_by(accs[f].reshape((r, accs[f].shape[0] // r) + accs[f].shape[1:]), d, r) for f in who]
            for f, sub in zip(who, subs):
                accs[f] = sub[0]
            for s in range(1, r):
                got = _exchange([sub[s] for sub in subs], axis, t, s)
                for f, g in zip(who, got):
                    accs[f] = accs[f] + g
    return [a[0] for a in accs]


def body(tensor, factor_first, factor_second, factor_third):
    nia, nja, nka = (lax.axis_size(a) for a in ("ia", "ja", "ka"))
    rows_i, rows_j, rows_k = tensor.shape
    c1, c2, c3 = factor_first.shape[1], factor_second.shape[1], factor_third.shape[1]
    rank = c1 * nja * nka
    g1, g2, g3 = gather_all([factor_first, factor_second, factor_third])
    full_first = g1.reshape(-1, rows_i, c1).transpose(1, 0, 2).reshape(rows_i, rank)
    full_second = g2.reshape(-1, rows_j, c2).transpose(1, 0, 2).reshape(rows_j, rank)
    full_third = g3.reshape(-1, rows_k, c3).transpose(1, 0, 2).reshape(rows_k, rank)

    total_i = rows_i * nia
    total_j = rows_j * nja
    total_k = rows_k * nka
    first32 = full_first.astype(jnp.float32)
    second32 = full_second.astype(jnp.float32)
    khatri = (first32[:, None, :] * second32[None, :, :]).astype(jnp.bfloat16)
    khatri_flat = khatri.reshape(rows_i * rows_j, rank)
    model = jnp.einsum("mr,kr->mk", khatri_flat, full_third, preferred_element_type=jnp.float32)
    flat_data = tensor.reshape(rows_i * rows_j, rows_k).astype(jnp.float32)
    deriv = ((model - flat_data) * lax.rsqrt(model)).astype(jnp.bfloat16)
    part_third = jnp.einsum("mk,mr->kr", deriv, khatri_flat, preferred_element_type=jnp.float32)
    inner = jnp.einsum("mk,kr->mr", deriv, full_third, preferred_element_type=jnp.float32)
    inner = inner.reshape(rows_i, rows_j, rank)
    part_first = jnp.sum(inner * second32[None, :, :], axis=1) / (total_j * total_k)
    part_second = jnp.sum(inner * first32[:, None, :], axis=0) / (total_i * total_k)
    part_third = part_third / (total_i * total_j)

    s1 = part_first.reshape(rows_i, nja * nka, c1).transpose(1, 0, 2)
    s2 = part_second.reshape(rows_j, nia * nka, c2).transpose(1, 0, 2)
    s3 = part_third.reshape(rows_k, nia * nja, c3).transpose(1, 0, 2)
    slots = [jnp.concatenate([_dense(blk) for blk in x]) for x in (s1, s2, s3)]
    g1, g2, g3 = reduce_all(slots)
    grad_first = g1.reshape(rows_i, c1)
    grad_second = g2.reshape(rows_j, c2)
    grad_third = g3.reshape(rows_k, c3)
    return (grad_first, grad_second, grad_third)


def solution(mesh):
    placed = (
        P("ia", "ja", "ka"),
        P("ia", ("ja", "ka")),
        P("ja", ("ia", "ka")),
        P("ka", ("ia", "ja")),
    )
    return jax.shard_map(
        body,
        mesh=mesh,
        in_specs=placed,
        out_specs=(P("ia", ("ja", "ka")), P("ja", ("ia", "ka")), P("ka", ("ia", "ja"))),
        check_vma=False,
    )
```

time: 57.2 us -> 51.6 us (0.902)
  other arithmetic: 5 us -> 1.08 us
  waiting for transfers between devices: 17.9 us -> 14.1 us
  local copies, waits for them, and re-layouts: 10.7 us -> 12.6 us
  matrix products: 2.75 us -> 4.31 us
  starting transfers between devices: 18.8 us -> 17.5 us
    another operation x0 -> x62, local copies, waits for them, and re-layouts: none -> 6.7 us  [the longest x32 2.6 us: _dense(): return flat.reshape(1, flat.shape[0] // lanes, lanes)]
    ppermute x10 -> x14, waiting for transfers between devices: 17.9 us -> 14.1 us  [_exchange(): got = lax.ppermute(payload, axis, [(i, i ^ s << t) for i in range(n)])]
    select_n x18, other arithmetic: 2.7 us -> 0.23 us  [_flip_by(): y = jnp.where(d // (1 << p) % 2 == 1, jnp.flip(y, w - 1 - p), y)]
    slice x38 -> x16, local copies, waits for them, and re-layouts: 2.22 us -> 0.05 us  [_exchange(): out.append(got[off:off + m].reshape(x.shape))]
    select_n x18 -> x0, local copies, waits for them, and re-layouts: 2.16 us -> none  [the longest x12 1.63 us: gather_all(): jnp.where(hi, jnp.concatenate([r, accs[f]]), jnp.concatenate([accs[f], r]))]
    reshape x23 -> x0, local copies, waits for them, and re-layouts: 2.09 us -> none  [the longest x10 1.09 us: _exchange(): flat = [x.reshape(-1) for x in items]]
    dot_general x1, matrix products: 0.87 us -> 2.41 us  [body(): jnp.einsum('mr,kr->mk', khatri_flat, full_third, preferred_element_type=j...]
    ppermute x10 -> x14, starting transfers between devices: 18.8 us -> 17.5 us  [_exchange(): got = lax.ppermute(payload, axis, [(i, i ^ s << t) for i in range(n)])]
  transfers between devices with their start and end apart: 10 -> 14, of which waited for: 10 -> 10; matrix products, arithmetic and copies ran while one was open for 5% -> 6% of each run, Pallas kernels for 0% -> 0%
where the time goes in v3:
time: 51.6 us; the launch traced here: 51.2 us
  starting transfers between devices  17.5 us (34%)
  waiting for transfers between devices  14.1 us (27%)
  local copies, waits for them, and re-layouts  12.6 us (24%)
  matrix products  4.31 us (8%)
  between operations  1.55 us (3%)
  other arithmetic  1.08 us (2%)
    ppermute x14, starting transfers between devices, _exchange(): got = lax.ppermute(payload, axis, [(i, i ^ s << t) for i in range(n)])  17.5 us
    ppermute x14, waiting for transfers between devices, _exchange(): got = lax.ppermute(payload, axis, [(i, i ^ s << t) for i in range(n)])  14.1 us
    unnamed x34, local copies, waits for them, and re-layouts  3.12 us
    another operation x32, local copies, waits for them, and re-layouts, _dense(): return flat.reshape(1, flat.shape[0] // lanes, lanes)  2.6 us
    dot_general x1, matrix products, body(): jnp.einsum('mr,kr->mk', khatri_flat, full_third, preferred_element_type=j...  2.41 us
    another operation x19, local copies, waits for them, and re-layouts, body(): slots = [jnp.concatenate([_dense(blk) for blk in x]) for x in (s1, s2, s3)]  2.04 us
  transfers between devices with their start and end apart: 14, of which 10 were waited for; matrix products, arithmetic and copies ran while one was open for 6% of the time, Pallas kernels for 0%

profile of v3, /device:TPU:0, one launch (start us, length us, event | category | flops | bytes accessed | tf_op | source)
XLA Modules:
  0.0 51.2 jit_solution(8245488327861415591)
XLA Ops:
  0.6 0.8 %copy.62 = bf16[128,16]{1,0:T(8,128)(2,1)S(1)} copy(bf16[128,16]{0,1:T(8,128)(2,1)} %param.6) | data formatting | bytes 8192 | tf_op args[2]
  1.5 0.8 %reshape_reshape_reshape.12 = bf16[1024]{0:T(1024)(128)(2,1)S(1)} reshape(bf16[32,32]{1,0:T(8,128)(2,1)} %param.5) | data formatting | bytes 4096 | tf_op jit(solution)/shard_map/reshape;reshape;reshape | solution.py:26
  2.3 5.1 %collective-permute-start.2 = (bf16[3072]{0:T(1024)(128)(2,1)S(1)}, bf16[3072]{0:T(1024)(128)(2,1)S(1)}, u32[]{:S(2)}, u32[]{:S(2)}) collective-permute-start(bf16[3072]{0:T(1024)(128)(2,1)S(1)} %constant_dynamic-update-slice_fusion.33), channel_id=1, source_target_pairs={{0,3},{1,2},{2,1},{3,0},{4,7},{5,6},{6,5},{7,4},{8,11},{9,10},{10,... | collective-permute-start | bytes 18440 | tf_op jit(solution)/shard_map/ppermute | solution.py:29
  7.4 0.6 %collective-permute-start = (bf16[3072]{0:T(1024)(128)(2,1)S(1)}, bf16[3072]{0:T(1024)(128)(2,1)S(1)}, u32[]{:S(2)}, u32[]{:S(2)}) collective-permute-start(bf16[3072]{0:T(1024)(128)(2,1)S(1)} %constant_dynamic-update-slice_fusion.33), channel_id=1, source_target_pairs={{0,1},{1,0},{2,3},{3,2},{4,5},{5,4},{6,7},{7,6},{8,9},{9,8},{10,11... | collective-permute-start | bytes 18440 | tf_op jit(solution)/shard_map/ppermute | solution.py:29
  8.1 0.8 %stack_reshape_reshape.15 = bf16[1,1,8,128]{3,2,1,0:T(8,128)(2,1)S(1)} reshape(bf16[32,32]{1,0:T(8,128)(2,1)} %param.5) | data formatting | bytes 4096 | tf_op jit(solution)/shard_map/stack;reshape;reshape | solution.py:61
  8.8 0.8 %copy.63 = bf16[256,32]{1,0:T(8,128)(2,1)S(1)} copy(bf16[256,32]{0,1:T(8,128)(2,1)} %param.7) | data formatting | bytes 32768 | tf_op args[3]
  10.0 1.9 %collective-permute-done.1 = bf16[3072]{0:T(1024)(128)(2,1)S(1)} collective-permute-done((bf16[3072]{0:T(1024)(128)(2,1)S(1)}, bf16[3072]{0:T(1024)(128)(2,1)S(1)}, u32[]{:S(2)}, u32[]{:S(2)}) %collective-permute-start.1) | collective-permute-done | bytes 6176 | tf_op jit(solution)/shard_map/ppermute | solution.py:29
  12.2 1.1 %collective-permute-done.3 = bf16[12288]{0:T(1024)(128)(2,1)S(1)} collective-permute-done((bf16[12288]{0:T(1024)(128)(2,1)S(1)}, bf16[12288]{0:T(1024)(128)(2,1)S(1)}, u32[]{:S(2)}, u32[]{:S(2)}) %collective-permute-start.3) | collective-permute-done | bytes 24608 | tf_op jit(solution)/shard_map/ppermute | solution.py:29
  13.3 1.6 %collective-permute-start.4 = (bf16[24576]{0:T(1024)(128)(2,1)S(1)}, bf16[24576]{0:T(1024)(128)(2,1)S(1)}, u32[]{:S(2)}, u32[]{:S(2)}) collective-permute-start(bf16[24576]{0:T(1024)(128)(2,1)S(1)} %pad_maximum_fusion.5), channel_id=1, source_target_pairs={{0,8},{8,0},{16,24},{24,16},{1,9},{9,1},{17,25},{25,17},{2,10},{10... | collective-permute-start | bytes 147464 | tf_op jit(solution)/shard_map/ppermute | solution.py:29
  14.9 1.5 %collective-permute-start.5 = (bf16[24576]{0:T(1024)(128)(2,1)S(1)}, bf16[24576]{0:T(1024)(128)(2,1)S(1)}, u32[]{:S(2)}, u32[]{:S(2)}) collective-permute-start(bf16[24576]{0:T(1024)(128)(2,1)S(1)} %pad_maximum_fusion.5), channel_id=1, source_target_pairs={{0,16},{8,24},{16,0},{24,8},{1,17},{9,25},{17,1},{25,9},{2,18},{10... | collective-permute-start | bytes 147464 | tf_op jit(solution)/shard_map/ppermute | solution.py:29
  16.4 0.5 collective-permute-start.6
  17.5 1.5 %collective-permute-done.5 = bf16[24576]{0:T(1024)(128)(2,1)S(1)} collective-permute-done((bf16[24576]{0:T(1024)(128)(2,1)S(1)}, bf16[24576]{0:T(1024)(128)(2,1)S(1)}, u32[]{:S(2)}, u32[]{:S(2)}) %collective-permute-start.5) | collective-permute-done | bytes 49184 | tf_op jit(solution)/shard_map/ppermute | solution.py:29
  19.0 2.4 %collective-permute-done.6 = bf16[24576]{0:T(1024)(128)(2,1)S(1)} collective-permute-done((bf16[24576]{0:T(1024)(128)(2,1)S(1)}, bf16[24576]{0:T(1024)(128)(2,1)S(1)}, u32[]{:S(2)}, u32[]{:S(2)}) %collective-permute-start.6) | collective-permute-done | bytes 49184 | tf_op jit(solution)/shard_map/ppermute | solution.py:29
  22.8 0.6 %multiply_convert_fusion = bf16[32,128,256]{2,1,0:T(8,128)(2,1)S(1)} fusion(f32[128,256]{1,0:T(8,128)S(1)} %copy.68, f32[32,256]{1,0:T(8,128)S(1)} %reshape.307), kind=kLoop, calls=%fused_computation.5 | loop fusion | flops 2097152 | bytes 2260992 | tf_op jit(solution)/shard_map/convert_element_type | solution.py:97
  23.4 2.4 %fusion.1 = bf16[4096,256]{1,0:T(8,128)(2,1)S(1)} fusion(bf16[32,128,256]{2,1,0:T(8,128)(2,1)} %param.4, bf16[4096,256]{1,0:T(8,128)(2,1)S(1)} %bitcast.175, bf16[256,256]{0,1:T(8,128)(2,1)S(1)} %bitcast.198), kind=kOutput, calls=%fused_computation.2 | convolution fusion | flops 541065216 | bytes 6422528 | tf_op jit(solution)/shard_map/mr,kr->mk/dot_general | solution.py:99
  25.8 1.0 %convolution_multiply_fusion = f32[256,256]{0,1:T(8,128)S(1)} fusion(bf16[4096,256]{1,0:T(8,128)(2,1)S(1)} %fusion.1, bf16[4096,256]{1,0:T(8,128)(2,1)S(1)} %bitcast.176), kind=kOutput, calls=%fused_computation.6 | convolution fusion | flops 536936448 | bytes 4456448 | tf_op jit(solution)/shard_map/mk,mr->kr/dot_general | solution.py:102
  26.8 0.9 %multiply_reduce_fusion.1 = (f32[32,256]{1,0:T(8,128)S(1)}, f32[128,256]{1,0:T(8,128)S(1)}) fusion(f32[128,256]{1,0:T(8,128)S(1)} %copy.68, f32[32,256]{1,0:T(8,128)S(1)} %reshape.307, bf16[32,128,256]{2,1,0:T(8,128)(2,1)S(1)} %bitcast.224, bf16[256,256,1]{0,1,2:T(8,128)(2,1)S(1)} %bitcast.199), kind=kOutput, calls=%fused_computation.4 | convolution fusion | flops 541024256 | bytes 2555904 | tf_op jit(solution)/shard_map/mk,kr->mr/dot_general | solution.py:103
  27.8 0.4 slice_reduce_fusion
  32.2 0.3 copy.71
  33.6 0.6 %collective-permute-start.7 = (f32[24576]{0:T(1024)S(1)}, f32[24576]{0:T(1024)S(1)}, u32[]{:S(2)}, u32[]{:S(2)}) collective-permute-start(f32[24576]{0:T(1024)S(1)} %pad_maximum_fusion.1), channel_id=1, source_target_pairs={{0,8},{8,0},{16,24},{24,16},{1,9},{9,1},{17,25},{25,17},{2,10},{10... | collective-permute-start | bytes 294920 | tf_op jit(solution)/shard_map/ppermute | solution.py:29
  34.2 0.6 %collective-permute-start.8 = (f32[24576]{0:T(1024)S(1)}, f32[24576]{0:T(1024)S(1)}, u32[]{:S(2)}, u32[]{:S(2)}) collective-permute-start(f32[24576]{0:T(1024)S(1)} %pad_maximum_fusion.2), channel_id=1, source_target_pairs={{0,16},{8,24},{16,0},{24,8},{1,17},{9,25},{17,1},{25,9},{2,18},{10... | collective-permute-start | bytes 294920 | tf_op jit(solution)/shard_map/ppermute | solution.py:29
  34.8 2.5 %collective-permute-start.9 = (f32[24576]{0:T(1024)S(1)}, f32[24576]{0:T(1024)S(1)}, u32[]{:S(2)}, u32[]{:S(2)}) collective-permute-start(f32[24576]{0:T(1024)S(1)} %pad_maximum_fusion.3), channel_id=1, source_target_pairs={{0,24},{8,16},{16,8},{24,0},{1,25},{9,17},{17,9},{25,1},{2,26},{10... | collective-permute-start | bytes 294920 | tf_op jit(solution)/shard_map/ppermute | solution.py:29
  37.3 1.1 %collective-permute-done.7 = f32[24576]{0:T(1024)S(1)} collective-permute-done((f32[24576]{0:T(1024)S(1)}, f32[24576]{0:T(1024)S(1)}, u32[]{:S(2)}, u32[]{:S(2)}) %collective-permute-start.7) | collective-permute-done | bytes 98336 | tf_op jit(solution)/shard_map/ppermute | solution.py:29
  38.4 0.5 collective-permute-done.8
  38.9 1.5 %collective-permute-done.9 = f32[24576]{0:T(1024)S(1)} collective-permute-done((f32[24576]{0:T(1024)S(1)}, f32[24576]{0:T(1024)S(1)}, u32[]{:S(2)}, u32[]{:S(2)}) %collective-permute-start.9) | collective-permute-done | bytes 98336 | tf_op jit(solution)/shard_map/ppermute | solution.py:29
  40.6 1.1 %collective-permute-done.10 = f32[12288]{0:T(1024)S(1)} collective-permute-done((f32[12288]{0:T(1024)S(1)}, f32[12288]{0:T(1024)S(1)}, u32[]{:S(2)}, u32[]{:S(2)}) %collective-permute-start.10) | collective-permute-done | bytes 49184 | tf_op jit(solution)/shard_map/ppermute | solution.py:29
  41.8 2.4 %collective-permute-start.12 = (f32[3072]{0:T(1024)S(1)}, f32[3072]{0:T(1024)S(1)}, u32[]{:S(2)}, u32[]{:S(2)}) collective-permute-start(f32[3072]{0:T(1024)S(1)} %pad_maximum_fusion.12), channel_id=1, source_target_pairs={{0,2},{1,3},{2,0},{3,1},{4,6},{5,7},{6,4},{7,5},{8,10},{9,11},{10,... | collective-permute-start | bytes 36872 | tf_op jit(solution)/shard_map/ppermute | solution.py:29
  44.2 2.0 %collective-permute-start.13 = (f32[3072]{0:T(1024)S(1)}, f32[3072]{0:T(1024)S(1)}, u32[]{:S(2)}, u32[]{:S(2)}) collective-permute-start(f32[3072]{0:T(1024)S(1)} %pad_maximum_fusion.13), channel_id=1, source_target_pairs={{0,3},{1,2},{2,1},{3,0},{4,7},{5,6},{6,5},{7,4},{8,11},{9,10},{10,... | collective-permute-start | bytes 36872 | tf_op jit(solution)/shard_map/ppermute | solution.py:29
  46.3 0.7 %copy.90 = f32[256,32]{0,1:T(8,128)} copy(f32[256,32]{1,0:T(8,128)S(1)} %reshape_squeeze.67) | data formatting | bytes 65536
  47.0 2.7 %collective-permute-done.13 = f32[3072]{0:T(1024)S(1)} collective-permute-done((f32[3072]{0:T(1024)S(1)}, f32[3072]{0:T(1024)S(1)}, u32[]{:S(2)}, u32[]{:S(2)}) %collective-permute-start.13) | collective-permute-done | bytes 12320 | tf_op jit(solution)/shard_map/ppermute | solution.py:29
  49.8 0.7 %copy.89 = f32[128,16]{0,1:T(8,128)} copy(f32[128,16]{1,0:T(8,128)S(1)} %reshape_squeeze.66) | data formatting | bytes 16384
  50.5 0.7 %reshape_squeeze.65 = f32[32,32]{1,0:T(8,128)} reshape(f32[8,128]{1,0:T(8,128)S(1)} %fusion.15) | data formatting | bytes 8192 | tf_op jit(solution)/shard_map/reshape;squeeze | solution.py:114
  (179 shorter events, 7.6 us)
Async XLA Ops:
  2.3 7.7 %collective-permute-start.2 = (bf16[3072]{0:T(1024)(128)(2,1)S(1)}, bf16[3072]{0:T(1024)(128)(2,1)S(1)}, u32[]{:S(2)}, u32[]{:S(2)}) collective-permute-start(bf16[3072]{0:T(1024)(128)(2,1)S(1)} %constant_dynamic-update-slice_fusion.33), channel_id=1, source_target_pairs={{0,3},{1,2},{2,1},{3,0},{4,7},{5,6},{6,5},{7,4},{8,11},{9,10},{10,... | collective-permute-start | bytes 18440 | tf_op jit(solution)/shard_map/ppermute | solution.py:29
  7.4 4.5 %collective-permute-start.1 = (bf16[3072]{0:T(1024)(128)(2,1)S(1)}, bf16[3072]{0:T(1024)(128)(2,1)S(1)}, u32[]{:S(2)}, u32[]{:S(2)}) collective-permute-start(bf16[3072]{0:T(1024)(128)(2,1)S(1)} %constant_dynamic-update-slice_fusion.33), channel_id=1, source_target_pairs={{0,2},{1,3},{2,0},{3,1},{4,6},{5,7},{6,4},{7,5},{8,10},{9,11},{10,... | collective-permute-start | bytes 18440 | tf_op jit(solution)/shard_map/ppermute | solution.py:29
  7.4 4.5 %collective-permute-start = (bf16[3072]{0:T(1024)(128)(2,1)S(1)}, bf16[3072]{0:T(1024)(128)(2,1)S(1)}, u32[]{:S(2)}, u32[]{:S(2)}) collective-permute-start(bf16[3072]{0:T(1024)(128)(2,1)S(1)} %constant_dynamic-update-slice_fusion.33), channel_id=1, source_target_pairs={{0,1},{1,0},{2,3},{3,2},{4,5},{5,4},{6,7},{7,6},{8,9},{9,8},{10,11... | collective-permute-start | bytes 18440 | tf_op jit(solution)/shard_map/ppermute | solution.py:29
  12.0 1.3 %collective-permute-start.3 = (bf16[12288]{0:T(1024)(128)(2,1)S(1)}, bf16[12288]{0:T(1024)(128)(2,1)S(1)}, u32[]{:S(2)}, u32[]{:S(2)}) collective-permute-start(bf16[12288]{0:T(1024)(128)(2,1)S(1)} %pad_maximum_fusion.8), channel_id=1, source_target_pairs={{0,4},{4,0},{1,5},{5,1},{2,6},{6,2},{3,7},{7,3},{8,12},{12,8},{9,1... | collective-permute-start | bytes 73736 | tf_op jit(solution)/shard_map/ppermute | solution.py:29
  13.3 4.2 %collective-permute-start.4 = (bf16[24576]{0:T(1024)(128)(2,1)S(1)}, bf16[24576]{0:T(1024)(128)(2,1)S(1)}, u32[]{:S(2)}, u32[]{:S(2)}) collective-permute-start(bf16[24576]{0:T(1024)(128)(2,1)S(1)} %pad_maximum_fusion.5), channel_id=1, source_target_pairs={{0,8},{8,0},{16,24},{24,16},{1,9},{9,1},{17,25},{25,17},{2,10},{10... | collective-permute-start | bytes 147464 | tf_op jit(solution)/shard_map/ppermute | solution.py:29
  14.9 4.1 %collective-permute-start.5 = (bf16[24576]{0:T(1024)(128)(2,1)S(1)}, bf16[24576]{0:T(1024)(128)(2,1)S(1)}, u32[]{:S(2)}, u32[]{:S(2)}) collective-permute-start(bf16[24576]{0:T(1024)(128)(2,1)S(1)} %pad_maximum_fusion.5), channel_id=1, source_target_pairs={{0,16},{8,24},{16,0},{24,8},{1,17},{9,25},{17,1},{25,9},{2,18},{10... | collective-permute-start | bytes 147464 | tf_op jit(solution)/shard_map/ppermute | solution.py:29
  16.4 5.0 %collective-permute-start.6 = (bf16[24576]{0:T(1024)(128)(2,1)S(1)}, bf16[24576]{0:T(1024)(128)(2,1)S(1)}, u32[]{:S(2)}, u32[]{:S(2)}) collective-permute-start(bf16[24576]{0:T(1024)(128)(2,1)S(1)} %pad_maximum_fusion.5), channel_id=1, source_target_pairs={{0,24},{8,16},{16,8},{24,0},{1,25},{9,17},{17,9},{25,1},{2,26},{10... | collective-permute-start | bytes 147464 | tf_op jit(solution)/shard_map/ppermute | solution.py:29
  33.6 4.8 %collective-permute-start.7 = (f32[24576]{0:T(1024)S(1)}, f32[24576]{0:T(1024)S(1)}, u32[]{:S(2)}, u32[]{:S(2)}) collective-permute-start(f32[24576]{0:T(1024)S(1)} %pad_maximum_fusion.1), channel_id=1, source_target_pairs={{0,8},{8,0},{16,24},{24,16},{1,9},{9,1},{17,25},{25,17},{2,10},{10... | collective-permute-start | bytes 294920 | tf_op jit(solution)/shard_map/ppermute | solution.py:29
  34.2 4.7 %collective-permute-start.8 = (f32[24576]{0:T(1024)S(1)}, f32[24576]{0:T(1024)S(1)}, u32[]{:S(2)}, u32[]{:S(2)}) collective-permute-start(f32[24576]{0:T(1024)S(1)} %pad_maximum_fusion.2), channel_id=1, source_target_pairs={{0,16},{8,24},{16,0},{24,8},{1,17},{9,25},{17,1},{25,9},{2,18},{10... | collective-permute-start | bytes 294920 | tf_op jit(solution)/shard_map/ppermute | solution.py:29
  34.8 5.6 %collective-permute-start.9 = (f32[24576]{0:T(1024)S(1)}, f32[24576]{0:T(1024)S(1)}, u32[]{:S(2)}, u32[]{:S(2)}) collective-permute-start(f32[24576]{0:T(1024)S(1)} %pad_maximum_fusion.3), channel_id=1, source_target_pairs={{0,24},{8,16},{16,8},{24,0},{1,25},{9,17},{17,9},{25,1},{2,26},{10... | collective-permute-start | bytes 294920 | tf_op jit(solution)/shard_map/ppermute | solution.py:29
  40.4 1.3 %collective-permute-start.10 = (f32[12288]{0:T(1024)S(1)}, f32[12288]{0:T(1024)S(1)}, u32[]{:S(2)}, u32[]{:S(2)}) collective-permute-start(f32[12288]{0:T(1024)S(1)} %pad_maximum_fusion.6), channel_id=1, source_target_pairs={{0,4},{4,0},{1,5},{5,1},{2,6},{6,2},{3,7},{7,3},{8,12},{12,8},{9,1... | collective-permute-start | bytes 147464 | tf_op jit(solution)/shard_map/ppermute | solution.py:29
  41.7 5.3 %collective-permute-start.11 = (f32[3072]{0:T(1024)S(1)}, f32[3072]{0:T(1024)S(1)}, u32[]{:S(2)}, u32[]{:S(2)}) collective-permute-start(f32[3072]{0:T(1024)S(1)} %pad_maximum_fusion.11), channel_id=1, source_target_pairs={{0,1},{1,0},{2,3},{3,2},{4,5},{5,4},{6,7},{7,6},{8,9},{9,8},{10,11... | collective-permute-start | bytes 36872 | tf_op jit(solution)/shard_map/ppermute | solution.py:29
  41.8 5.2 %collective-permute-start.12 = (f32[3072]{0:T(1024)S(1)}, f32[3072]{0:T(1024)S(1)}, u32[]{:S(2)}, u32[]{:S(2)}) collective-permute-start(f32[3072]{0:T(1024)S(1)} %pad_maximum_fusion.12), channel_id=1, source_target_pairs={{0,2},{1,3},{2,0},{3,1},{4,6},{5,7},{6,4},{7,5},{8,10},{9,11},{10,... | collective-permute-start | bytes 36872 | tf_op jit(solution)/shard_map/ppermute | solution.py:29
  44.2 5.5 %collective-permute-start.13 = (f32[3072]{0:T(1024)S(1)}, f32[3072]{0:T(1024)S(1)}, u32[]{:S(2)}, u32[]{:S(2)}) collective-permute-start(f32[3072]{0:T(1024)S(1)} %pad_maximum_fusion.13), channel_id=1, source_target_pairs={{0,3},{1,2},{2,1},{3,0},{4,7},{5,6},{6,5},{7,4},{8,11},{9,10},{10,... | collective-permute-start | bytes 36872 | tf_op jit(solution)/shard_map/ppermute | solution.py:29

commit v4 on v3

--- a/solution.py
+++ b/solution.py
@@ -109,7 +109,7 @@
     s1 = part_first.reshape(rows_i, nja * nka, c1).transpose(1, 0, 2)
     s2 = part_second.reshape(rows_j, nia * nka, c2).transpose(1, 0, 2)
     s3 = part_third.reshape(rows_k, nia * nja, c3).transpose(1, 0, 2)
-    slots = [jnp.concatenate([_dense(blk) for blk in x]) for x in (s1, s2, s3)]
+    slots = [x.reshape((x.shape[0],) + _dense(x[0]).shape[1:]) for x in (s1, s2, s3)]
     g1, g2, g3 = reduce_all(slots)
     grad_first = g1.reshape(rows_i, c1)
     grad_second = g2.reshape(rows_j, c2)

time: 51.6 us -> 45.8 us (0.89)
  local copies, waits for them, and re-layouts: 12.6 us -> 8.85 us
  waiting for transfers between devices: 14.1 us -> 12.4 us
    another operation x51 -> x3, local copies, waits for them, and re-layouts: 4.64 us -> 0.67 us  [the longest x2 0.59 us: _flip_by(): y = x.reshape((2,) * w + rest)]
    ppermute x14, waiting for transfers between devices: 14.1 us -> 12.4 us  [_exchange(): got = lax.ppermute(payload, axis, [(i, i ^ s << t) for i in range(n)])]
    unnamed x34 -> x5, local copies, waits for them, and re-layouts: 3.12 us -> 3.02 us
  transfers between devices with their start and end apart: 14 -> 14, of which waited for: 10 -> 11; matrix products, arithmetic and copies ran while one was open for 6% -> 7% of each run, Pallas kernels for 0% -> 0%
where the time goes in v4:
time: 45.8 us; the launch traced here: 45.4 us
  starting transfers between devices  17.6 us (38%)
  waiting for transfers between devices  12.4 us (27%)
  local copies, waits for them, and re-layouts  8.85 us (19%)
  matrix products  4.31 us (9%)
  between operations  1.25 us (3%)
  other arithmetic  1.08 us (2%)
    ppermute x14, starting transfers between devices, _exchange(): got = lax.ppermute(payload, axis, [(i, i ^ s << t) for i in range(n)])  17.6 us
    ppermute x14, waiting for transfers between devices, _exchange(): got = lax.ppermute(payload, axis, [(i, i ^ s << t) for i in range(n)])  12.4 us
    unnamed x5, local copies, waits for them, and re-layouts  3.02 us
    dot_general x1, matrix products, body(): jnp.einsum('mr,kr->mk', khatri_flat, full_third, preferred_element_type=j...  2.42 us
    another operation x7, local copies, waits for them, and re-layouts, _exchange(): flat = [x.reshape(-1) for x in items]  0.99 us
    another operation x7, local copies, waits for them, and re-layouts, gather_all(): cands = _flip_by(jnp.stack([mine[i]] + [g[i] for g in got]), d, r)  0.98 us
    dot_general x1, matrix products, body(): jnp.einsum('mk,mr->kr', deriv, khatri_flat, preferred_element_type=jnp.fl...  0.96 us
    dot_general x1, matrix products, body(): jnp.einsum('mk,kr->mr', deriv, full_third, preferred_element_type=jnp.flo...  0.93 us
  transfers between devices with their start and end apart: 14, of which 11 were waited for; matrix products, arithmetic and copies ran while one was open for 7% of the time, Pallas kernels for 0%

profile of v4, /device:TPU:0, one launch (start us, length us, event | category | flops | bytes accessed | tf_op | source)
XLA Modules:
  0.0 45.4 jit_solution(13068680350353612250)
XLA Ops:
  0.6 0.8 %reshape_reshape_reshape.31 = bf16[1024]{0:T(1024)(128)(2,1)S(1)} reshape(bf16[32,32]{1,0:T(8,128)(2,1)} %param.5) | data formatting | bytes 4096 | tf_op jit(solution)/shard_map/reshape;reshape;reshape | solution.py:26
  1.4 0.8 %copy.34 = bf16[128,16]{1,0:T(8,128)(2,1)S(1)} copy(bf16[128,16]{0,1:T(8,128)(2,1)} %param.6) | data formatting | bytes 8192 | tf_op args[2]
  2.3 5.1 %collective-permute-start.2 = (bf16[3072]{0:T(1024)(128)(2,1)S(1)}, bf16[3072]{0:T(1024)(128)(2,1)S(1)}, u32[]{:S(2)}, u32[]{:S(2)}) collective-permute-start(bf16[3072]{0:T(1024)(128)(2,1)S(1)} %constant_dynamic-update-slice_fusion), channel_id=1, source_target_pairs={{0,3},{1,2},{2,1},{3,0},{4,7},{5,6},{6,5},{7,4},{8,11},{9,10},{10,... | collective-permute-start | bytes 18440 | tf_op jit(solution)/shard_map/ppermute | solution.py:29
  7.4 0.6 %collective-permute-start = (bf16[3072]{0:T(1024)(128)(2,1)S(1)}, bf16[3072]{0:T(1024)(128)(2,1)S(1)}, u32[]{:S(2)}, u32[]{:S(2)}) collective-permute-start(bf16[3072]{0:T(1024)(128)(2,1)S(1)} %constant_dynamic-update-slice_fusion), channel_id=1, source_target_pairs={{0,1},{1,0},{2,3},{3,2},{4,5},{5,4},{6,7},{7,6},{8,9},{9,8},{10,11... | collective-permute-start | bytes 18440 | tf_op jit(solution)/shard_map/ppermute | solution.py:29
  8.1 0.8 %stack_reshape_reshape.15 = bf16[1,1,8,128]{3,2,1,0:T(8,128)(2,1)S(1)} reshape(bf16[32,32]{1,0:T(8,128)(2,1)} %param.5) | data formatting | bytes 4096 | tf_op jit(solution)/shard_map/stack;reshape;reshape | solution.py:61
  9.0 0.8 %copy.35 = bf16[256,32]{1,0:T(8,128)(2,1)S(1)} copy(bf16[256,32]{0,1:T(8,128)(2,1)} %param.7) | data formatting | bytes 32768 | tf_op args[3]
  10.1 1.9 %collective-permute-done.1 = bf16[3072]{0:T(1024)(128)(2,1)S(1)} collective-permute-done((bf16[3072]{0:T(1024)(128)(2,1)S(1)}, bf16[3072]{0:T(1024)(128)(2,1)S(1)}, u32[]{:S(2)}, u32[]{:S(2)}) %collective-permute-start.1) | collective-permute-done | bytes 6176 | tf_op jit(solution)/shard_map/ppermute | solution.py:29
  12.2 1.2 %collective-permute-done.3 = bf16[12288]{0:T(1024)(128)(2,1)S(1)} collective-permute-done((bf16[12288]{0:T(1024)(128)(2,1)S(1)}, bf16[12288]{0:T(1024)(128)(2,1)S(1)}, u32[]{:S(2)}, u32[]{:S(2)}) %collective-permute-start.3) | collective-permute-done | bytes 24608 | tf_op jit(solution)/shard_map/ppermute | solution.py:29
  13.4 2.5 %collective-permute-start.6 = (bf16[24576]{0:T(1024)(128)(2,1)S(1)}, bf16[24576]{0:T(1024)(128)(2,1)S(1)}, u32[]{:S(2)}, u32[]{:S(2)}) collective-permute-start(bf16[24576]{0:T(1024)(128)(2,1)S(1)} %pad_maximum_fusion.5), channel_id=1, source_target_pairs={{0,24},{8,16},{16,8},{24,0},{1,25},{9,17},{17,9},{25,1},{2,26},{10... | collective-permute-start | bytes 147464 | tf_op jit(solution)/shard_map/ppermute | solution.py:29
  15.9 0.5 %collective-permute-start.5 = (bf16[24576]{0:T(1024)(128)(2,1)S(1)}, bf16[24576]{0:T(1024)(128)(2,1)S(1)}, u32[]{:S(2)}, u32[]{:S(2)}) collective-permute-start(bf16[24576]{0:T(1024)(128)(2,1)S(1)} %pad_maximum_fusion.5), channel_id=1, source_target_pairs={{0,16},{8,24},{16,0},{24,8},{1,17},{9,25},{17,1},{25,9},{2,18},{10... | collective-permute-start | bytes 147464 | tf_op jit(solution)/shard_map/ppermute | solution.py:29
  16.4 0.5 %collective-permute-start.4 = (bf16[24576]{0:T(1024)(128)(2,1)S(1)}, bf16[24576]{0:T(1024)(128)(2,1)S(1)}, u32[]{:S(2)}, u32[]{:S(2)}) collective-permute-start(bf16[24576]{0:T(1024)(128)(2,1)S(1)} %pad_maximum_fusion.5), channel_id=1, source_target_pairs={{0,8},{8,0},{16,24},{24,16},{1,9},{9,1},{17,25},{25,17},{2,10},{10... | collective-permute-start | bytes 147464 | tf_op jit(solution)/shard_map/ppermute | solution.py:29
  17.3 1.2 %collective-permute-done.6 = bf16[24576]{0:T(1024)(128)(2,1)S(1)} collective-permute-done((bf16[24576]{0:T(1024)(128)(2,1)S(1)}, bf16[24576]{0:T(1024)(128)(2,1)S(1)}, u32[]{:S(2)}, u32[]{:S(2)}) %collective-permute-start.6) | collective-permute-done | bytes 49184 | tf_op jit(solution)/shard_map/ppermute | solution.py:29
  18.5 1.5 %collective-permute-done.5 = bf16[24576]{0:T(1024)(128)(2,1)S(1)} collective-permute-done((bf16[24576]{0:T(1024)(128)(2,1)S(1)}, bf16[24576]{0:T(1024)(128)(2,1)S(1)}, u32[]{:S(2)}, u32[]{:S(2)}) %collective-permute-start.5) | collective-permute-done | bytes 49184 | tf_op jit(solution)/shard_map/ppermute | solution.py:29
  20.0 0.5 %collective-permute-done.4 = bf16[24576]{0:T(1024)(128)(2,1)S(1)} collective-permute-done((bf16[24576]{0:T(1024)(128)(2,1)S(1)}, bf16[24576]{0:T(1024)(128)(2,1)S(1)}, u32[]{:S(2)}, u32[]{:S(2)}) %collective-permute-start.4) | collective-permute-done | bytes 49184 | tf_op jit(solution)/shard_map/ppermute | solution.py:29
  21.9 0.6 %multiply_convert_fusion = bf16[32,128,256]{2,1,0:T(8,128)(2,1)S(1)} fusion(f32[128,256]{1,0:T(8,128)S(1)} %copy.40, f32[32,256]{1,0:T(8,128)S(1)} %reshape.303), kind=kLoop, calls=%fused_computation.5 | loop fusion | flops 2097152 | bytes 2260992 | tf_op jit(solution)/shard_map/convert_element_type | solution.py:97
  22.5 2.4 %fusion.1 = bf16[4096,256]{1,0:T(8,128)(2,1)S(1)} fusion(bf16[32,128,256]{2,1,0:T(8,128)(2,1)} %param.4, bf16[4096,256]{1,0:T(8,128)(2,1)S(1)} %bitcast.174, bf16[256,256]{0,1:T(8,128)(2,1)S(1)} %bitcast.195), kind=kOutput, calls=%fused_computation.2 | convolution fusion | flops 541065216 | bytes 6422528 | tf_op jit(solution)/shard_map/mr,kr->mk/dot_general | solution.py:99
  25.0 1.0 %convolution_multiply_fusion = f32[256,256]{0,1:T(8,128)S(1)} fusion(bf16[4096,256]{1,0:T(8,128)(2,1)S(1)} %fusion.1, bf16[4096,256]{1,0:T(8,128)(2,1)S(1)} %bitcast.175), kind=kOutput, calls=%fused_computation.6 | convolution fusion | flops 536936448 | bytes 4456448 | tf_op jit(solution)/shard_map/mk,mr->kr/dot_general | solution.py:102
  25.9 0.9 %multiply_reduce_fusion.1 = (f32[32,256]{1,0:T(8,128)S(1)}, f32[128,256]{1,0:T(8,128)S(1)}) fusion(f32[128,256]{1,0:T(8,128)S(1)} %copy.40, f32[32,256]{1,0:T(8,128)S(1)} %reshape.303, bf16[32,128,256]{2,1,0:T(8,128)(2,1)S(1)} %bitcast.220, bf16[256,256,1]{0,1,2:T(8,128)(2,1)S(1)} %bitcast.196), kind=kOutput, calls=%fused_computation.4 | convolution fusion | flops 541024256 | bytes 2555904 | tf_op jit(solution)/shard_map/mk,kr->mr/dot_general | solution.py:103
  27.2 0.3 copy.44
  28.7 1.6 %collective-permute-start.8 = (f32[24576]{0:T(1024)S(1)}, f32[24576]{0:T(1024)S(1)}, u32[]{:S(2)}, u32[]{:S(2)}) collective-permute-start(f32[24576]{0:T(1024)S(1)} %pad_maximum_fusion.2), channel_id=1, source_target_pairs={{0,16},{8,24},{16,0},{24,8},{1,17},{9,25},{17,1},{25,9},{2,18},{10... | collective-permute-start | bytes 294920 | tf_op jit(solution)/shard_map/ppermute | solution.py:29
  30.3 0.5 %collective-permute-start.9 = (f32[24576]{0:T(1024)S(1)}, f32[24576]{0:T(1024)S(1)}, u32[]{:S(2)}, u32[]{:S(2)}) collective-permute-start(f32[24576]{0:T(1024)S(1)} %pad_maximum_fusion.3), channel_id=1, source_target_pairs={{0,24},{8,16},{16,8},{24,0},{1,25},{9,17},{17,9},{25,1},{2,26},{10... | collective-permute-start | bytes 294920 | tf_op jit(solution)/shard_map/ppermute | solution.py:29
  30.8 1.6 %collective-permute-start.7 = (f32[24576]{0:T(1024)S(1)}, f32[24576]{0:T(1024)S(1)}, u32[]{:S(2)}, u32[]{:S(2)}) collective-permute-start(f32[24576]{0:T(1024)S(1)} %pad_maximum_fusion.1), channel_id=1, source_target_pairs={{0,8},{8,0},{16,24},{24,16},{1,9},{9,1},{17,25},{25,17},{2,10},{10... | collective-permute-start | bytes 294920 | tf_op jit(solution)/shard_map/ppermute | solution.py:29
  32.4 2.0 %collective-permute-done.8 = f32[24576]{0:T(1024)S(1)} collective-permute-done((f32[24576]{0:T(1024)S(1)}, f32[24576]{0:T(1024)S(1)}, u32[]{:S(2)}, u32[]{:S(2)}) %collective-permute-start.8) | collective-permute-done | bytes 98336 | tf_op jit(solution)/shard_map/ppermute | solution.py:29
  34.4 1.4 %collective-permute-done.9 = f32[24576]{0:T(1024)S(1)} collective-permute-done((f32[24576]{0:T(1024)S(1)}, f32[24576]{0:T(1024)S(1)}, u32[]{:S(2)}, u32[]{:S(2)}) %collective-permute-start.9) | collective-permute-done | bytes 98336 | tf_op jit(solution)/shard_map/ppermute | solution.py:29
  36.2 1.2 %collective-permute-done.10 = f32[12288]{0:T(1024)S(1)} collective-permute-done((f32[12288]{0:T(1024)S(1)}, f32[12288]{0:T(1024)S(1)}, u32[]{:S(2)}, u32[]{:S(2)}) %collective-permute-start.10) | collective-permute-done | bytes 49184 | tf_op jit(solution)/shard_map/ppermute | solution.py:29
  37.4 2.0 %collective-permute-start.13 = (f32[3072]{0:T(1024)S(1)}, f32[3072]{0:T(1024)S(1)}, u32[]{:S(2)}, u32[]{:S(2)}) collective-permute-start(f32[3072]{0:T(1024)S(1)} %pad_maximum_fusion.13), channel_id=1, source_target_pairs={{0,3},{1,2},{2,1},{3,0},{4,7},{5,6},{6,5},{7,4},{8,11},{9,10},{10,... | collective-permute-start | bytes 36872 | tf_op jit(solution)/shard_map/ppermute | solution.py:29
  39.6 2.3 %collective-permute-start.11 = (f32[3072]{0:T(1024)S(1)}, f32[3072]{0:T(1024)S(1)}, u32[]{:S(2)}, u32[]{:S(2)}) collective-permute-start(f32[3072]{0:T(1024)S(1)} %pad_maximum_fusion.11), channel_id=1, source_target_pairs={{0,1},{1,0},{2,3},{3,2},{4,5},{5,4},{6,7},{7,6},{8,9},{9,8},{10,11... | collective-permute-start | bytes 36872 | tf_op jit(solution)/shard_map/ppermute | solution.py:29
  42.0 0.7 %copy.49 = f32[256,32]{0,1:T(8,128)} copy(f32[256,32]{1,0:T(8,128)S(1)} %reshape_squeeze.67) | data formatting | bytes 65536
  42.7 0.4 collective-permute-done.13
  43.1 0.9 %collective-permute-done.12 = f32[3072]{0:T(1024)S(1)} collective-permute-done((f32[3072]{0:T(1024)S(1)}, f32[3072]{0:T(1024)S(1)}, u32[]{:S(2)}, u32[]{:S(2)}) %collective-permute-start.12) | collective-permute-done | bytes 12320 | tf_op jit(solution)/shard_map/ppermute | solution.py:29
  44.0 0.7 %reshape_squeeze.65 = f32[32,32]{1,0:T(8,128)} reshape(f32[8,128]{1,0:T(8,128)S(1)} %fusion.15) | data formatting | bytes 8192 | tf_op jit(solution)/shard_map/reshape;squeeze | solution.py:114
  44.8 0.7 %copy.48 = f32[128,16]{0,1:T(8,128)} copy(f32[128,16]{1,0:T(8,128)S(1)} %reshape_squeeze.66) | data formatting | bytes 16384
  (101 shorter events, 4.2 us)
Async XLA Ops:
  2.3 7.7 %collective-permute-start.2 = (bf16[3072]{0:T(1024)(128)(2,1)S(1)}, bf16[3072]{0:T(1024)(128)(2,1)S(1)}, u32[]{:S(2)}, u32[]{:S(2)}) collective-permute-start(bf16[3072]{0:T(1024)(128)(2,1)S(1)} %constant_dynamic-update-slice_fusion), channel_id=1, source_target_pairs={{0,3},{1,2},{2,1},{3,0},{4,7},{5,6},{6,5},{7,4},{8,11},{9,10},{10,... | collective-permute-start | bytes 18440 | tf_op jit(solution)/shard_map/ppermute | solution.py:29
  7.4 4.5 %collective-permute-start.1 = (bf16[3072]{0:T(1024)(128)(2,1)S(1)}, bf16[3072]{0:T(1024)(128)(2,1)S(1)}, u32[]{:S(2)}, u32[]{:S(2)}) collective-permute-start(bf16[3072]{0:T(1024)(128)(2,1)S(1)} %constant_dynamic-update-slice_fusion), channel_id=1, source_target_pairs={{0,2},{1,3},{2,0},{3,1},{4,6},{5,7},{6,4},{7,5},{8,10},{9,11},{10,... | collective-permute-start | bytes 18440 | tf_op jit(solution)/shard_map/ppermute | solution.py:29
  7.4 4.5 %collective-permute-start = (bf16[3072]{0:T(1024)(128)(2,1)S(1)}, bf16[3072]{0:T(1024)(128)(2,1)S(1)}, u32[]{:S(2)}, u32[]{:S(2)}) collective-permute-start(bf16[3072]{0:T(1024)(128)(2,1)S(1)} %constant_dynamic-update-slice_fusion), channel_id=1, source_target_pairs={{0,1},{1,0},{2,3},{3,2},{4,5},{5,4},{6,7},{7,6},{8,9},{9,8},{10,11... | collective-permute-start | bytes 18440 | tf_op jit(solution)/shard_map/ppermute | solution.py:29
  12.1 1.3 %collective-permute-start.3 = (bf16[12288]{0:T(1024)(128)(2,1)S(1)}, bf16[12288]{0:T(1024)(128)(2,1)S(1)}, u32[]{:S(2)}, u32[]{:S(2)}) collective-permute-start(bf16[12288]{0:T(1024)(128)(2,1)S(1)} %pad_maximum_fusion.8), channel_id=1, source_target_pairs={{0,4},{4,0},{1,5},{5,1},{2,6},{6,2},{3,7},{7,3},{8,12},{12,8},{9,1... | collective-permute-start | bytes 73736 | tf_op jit(solution)/shard_map/ppermute | solution.py:29
  13.4 5.1 %collective-permute-start.6 = (bf16[24576]{0:T(1024)(128)(2,1)S(1)}, bf16[24576]{0:T(1024)(128)(2,1)S(1)}, u32[]{:S(2)}, u32[]{:S(2)}) collective-permute-start(bf16[24576]{0:T(1024)(128)(2,1)S(1)} %pad_maximum_fusion.5), channel_id=1, source_target_pairs={{0,24},{8,16},{16,8},{24,0},{1,25},{9,17},{17,9},{25,1},{2,26},{10... | collective-permute-start | bytes 147464 | tf_op jit(solution)/shard_map/ppermute | solution.py:29
  15.9 4.1 %collective-permute-start.5 = (bf16[24576]{0:T(1024)(128)(2,1)S(1)}, bf16[24576]{0:T(1024)(128)(2,1)S(1)}, u32[]{:S(2)}, u32[]{:S(2)}) collective-permute-start(bf16[24576]{0:T(1024)(128)(2,1)S(1)} %pad_maximum_fusion.5), channel_id=1, source_target_pairs={{0,16},{8,24},{16,0},{24,8},{1,17},{9,25},{17,1},{25,9},{2,18},{10... | collective-permute-start | bytes 147464 | tf_op jit(solution)/shard_map/ppermute | solution.py:29
  16.4 4.1 %collective-permute-start.4 = (bf16[24576]{0:T(1024)(128)(2,1)S(1)}, bf16[24576]{0:T(1024)(128)(2,1)S(1)}, u32[]{:S(2)}, u32[]{:S(2)}) collective-permute-start(bf16[24576]{0:T(1024)(128)(2,1)S(1)} %pad_maximum_fusion.5), channel_id=1, source_target_pairs={{0,8},{8,0},{16,24},{24,16},{1,9},{9,1},{17,25},{25,17},{2,10},{10... | collective-permute-start | bytes 147464 | tf_op jit(solution)/shard_map/ppermute | solution.py:29
  28.7 5.7 %collective-permute-start.8 = (f32[24576]{0:T(1024)S(1)}, f32[24576]{0:T(1024)S(1)}, u32[]{:S(2)}, u32[]{:S(2)}) collective-permute-start(f32[24576]{0:T(1024)S(1)} %pad_maximum_fusion.2), channel_id=1, source_target_pairs={{0,16},{8,24},{16,0},{24,8},{1,17},{9,25},{17,1},{25,9},{2,18},{10... | collective-permute-start | bytes 294920 | tf_op jit(solution)/shard_map/ppermute | solution.py:29
  30.3 5.6 %collective-permute-start.9 = (f32[24576]{0:T(1024)S(1)}, f32[24576]{0:T(1024)S(1)}, u32[]{:S(2)}, u32[]{:S(2)}) collective-permute-start(f32[24576]{0:T(1024)S(1)} %pad_maximum_fusion.3), channel_id=1, source_target_pairs={{0,24},{8,16},{16,8},{24,0},{1,25},{9,17},{17,9},{25,1},{2,26},{10... | collective-permute-start | bytes 294920 | tf_op jit(solution)/shard_map/ppermute | solution.py:29
  30.8 5.1 %collective-permute-start.7 = (f32[24576]{0:T(1024)S(1)}, f32[24576]{0:T(1024)S(1)}, u32[]{:S(2)}, u32[]{:S(2)}) collective-permute-start(f32[24576]{0:T(1024)S(1)} %pad_maximum_fusion.1), channel_id=1, source_target_pairs={{0,8},{8,0},{16,24},{24,16},{1,9},{9,1},{17,25},{25,17},{2,10},{10... | collective-permute-start | bytes 294920 | tf_op jit(solution)/shard_map/ppermute | solution.py:29
  36.1 1.3 %collective-permute-start.10 = (f32[12288]{0:T(1024)S(1)}, f32[12288]{0:T(1024)S(1)}, u32[]{:S(2)}, u32[]{:S(2)}) collective-permute-start(f32[12288]{0:T(1024)S(1)} %pad_maximum_fusion.6), channel_id=1, source_target_pairs={{0,4},{4,0},{1,5},{5,1},{2,6},{6,2},{3,7},{7,3},{8,12},{12,8},{9,1... | collective-permute-start | bytes 147464 | tf_op jit(solution)/shard_map/ppermute | solution.py:29
  37.4 5.7 %collective-permute-start.13 = (f32[3072]{0:T(1024)S(1)}, f32[3072]{0:T(1024)S(1)}, u32[]{:S(2)}, u32[]{:S(2)}) collective-permute-start(f32[3072]{0:T(1024)S(1)} %pad_maximum_fusion.13), channel_id=1, source_target_pairs={{0,3},{1,2},{2,1},{3,0},{4,7},{5,6},{6,5},{7,4},{8,11},{9,10},{10,... | collective-permute-start | bytes 36872 | tf_op jit(solution)/shard_map/ppermute | solution.py:29
  39.4 4.6 %collective-permute-start.12 = (f32[3072]{0:T(1024)S(1)}, f32[3072]{0:T(1024)S(1)}, u32[]{:S(2)}, u32[]{:S(2)}) collective-permute-start(f32[3072]{0:T(1024)S(1)} %pad_maximum_fusion.12), channel_id=1, source_target_pairs={{0,2},{1,3},{2,0},{3,1},{4,6},{5,7},{6,4},{7,5},{8,10},{9,11},{10,... | collective-permute-start | bytes 36872 | tf_op jit(solution)/shard_map/ppermute | solution.py:29
  39.6 4.4 %collective-permute-start.11 = (f32[3072]{0:T(1024)S(1)}, f32[3072]{0:T(1024)S(1)}, u32[]{:S(2)}, u32[]{:S(2)}) collective-permute-start(f32[3072]{0:T(1024)S(1)} %pad_maximum_fusion.11), channel_id=1, source_target_pairs={{0,1},{1,0},{2,3},{3,2},{4,5},{5,4},{6,7},{7,6},{8,9},{9,8},{10,11... | collective-permute-start | bytes 36872 | tf_op jit(solution)/shard_map/ppermute | solution.py:29

commit v5 on v4

--- a/solution.py
+++ b/solution.py
@@ -84,10 +84,10 @@
     rows_i, rows_j, rows_k = tensor.shape
     c1, c2, c3 = factor_first.shape[1], factor_second.shape[1], factor_third.shape[1]
     rank = c1 * nja * nka
-    g1, g2, g3 = gather_all([factor_first, factor_second, factor_third])
+    g1, g2, g3 = gather_all([factor_first, factor_second.T, factor_third.T])
     full_first = g1.reshape(-1, rows_i, c1).transpose(1, 0, 2).reshape(rows_i, rank)
-    full_second = g2.reshape(-1, rows_j, c2).transpose(1, 0, 2).reshape(rows_j, rank)
-    full_third = g3.reshape(-1, rows_k, c3).transpose(1, 0, 2).reshape(rows_k, rank)
+    full_second = g2.reshape(rank, rows_j).T
+    full_third = g3.reshape(rank, rows_k).T
 
     total_i = rows_i * nia
     total_j = rows_j * nja
@@ -107,13 +107,13 @@
     part_third = part_third / (total_i * total_j)
 
     s1 = part_first.reshape(rows_i, nja * nka, c1).transpose(1, 0, 2)
-    s2 = part_second.reshape(rows_j, nia * nka, c2).transpose(1, 0, 2)
-    s3 = part_third.reshape(rows_k, nia * nja, c3).transpose(1, 0, 2)
+    s2 = part_second.reshape(rows_j, nia * nka, c2).transpose(1, 2, 0)
+    s3 = part_third.reshape(rows_k, nia * nja, c3).transpose(1, 2, 0)
     slots = [x.reshape((x.shape[0],) + _dense(x[0]).shape[1:]) for x in (s1, s2, s3)]
     g1, g2, g3 = reduce_all(slots)
     grad_first = g1.reshape(rows_i, c1)
-    grad_second = g2.reshape(rows_j, c2)
-    grad_third = g3.reshape(rows_k, c3)
+    grad_second = g2.reshape(c2, rows_j).T
+    grad_third = g3.reshape(c3, rows_k).T
     return (grad_first, grad_second, grad_third)
 
 

time: 45.8 us -> 44.1 us (0.963)
  local copies, waits for them, and re-layouts: 8.85 us -> 5.72 us
  other arithmetic: 1.08 us -> 3.09 us
  matrix products: 4.31 us -> 2.75 us
  waiting for transfers between devices: 12.4 us -> 13.5 us
    unnamed x5 -> x3, local copies, waits for them, and re-layouts: 3.02 us -> 1.26 us
    dot_general x1, matrix products: 2.42 us -> 0.87 us  [body(): jnp.einsum('mr,kr->mk', khatri_flat, full_third, preferred_element_type=j...]
    ppermute x14, waiting for transfers between devices: 12.4 us -> 13.5 us  [_exchange(): got = lax.ppermute(payload, axis, [(i, i ^ s << t) for i in range(n)])]
    concatenate x9 -> x10, other arithmetic: 0.05 us -> 0.74 us  [_exchange(): payload = jnp.concatenate(flat) if len(flat) > 1 else flat[0]]
    another operation x7, other arithmetic: 0.07 us -> 0.76 us  [gather_all(): cands = _flip_by(jnp.stack([mine[i]] + [g[i] for g in got]), d, r)]
    convert_element_type x3 -> x1, local copies, waits for them, and re-layouts: 0.72 us -> 0.09 us  [body(): second32 = full_second.astype(jnp.float32)]
    transpose x0 -> x1, other arithmetic: none -> 0.6 us  [body(): grad_second = g2.reshape(c2, rows_j).T]
    another operation x2 -> x1, local copies, waits for them, and re-layouts: 0.59 us -> 0.02 us  [_flip_by(): y = x.reshape((2,) * w + rest)]
  transfers between devices with their start and end apart: 14 -> 14, of which waited for: 11 -> 10; matrix products, arithmetic and copies ran while one was open for 7% -> 10% of each run, Pallas kernels for 0% -> 0%
where the time goes in v5:
time: 44.1 us; the launch traced here: 43.6 us
  starting transfers between devices  17.4 us (39%)
  waiting for transfers between devices  13.5 us (31%)
  local copies, waits for them, and re-layouts  5.72 us (13%)
  other arithmetic  3.09 us (7%)
  matrix products  2.75 us (6%)
  between operations  1.17 us (3%)
    ppermute x14, starting transfers between devices, _exchange(): got = lax.ppermute(payload, axis, [(i, i ^ s << t) for i in range(n)])  17.4 us
    ppermute x14, waiting for transfers between devices, _exchange(): got = lax.ppermute(payload, axis, [(i, i ^ s << t) for i in range(n)])  13.5 us
    another operation x6, local copies, waits for them, and re-layouts, gather_all(): cands = _flip_by(jnp.stack([mine[i]] + [g[i] for g in got]), d, r)  1.52 us
    unnamed x3, local copies, waits for them, and re-layouts  1.26 us
    dot_general x1, matrix products, body(): jnp.einsum('mk,mr->kr', deriv, khatri_flat, preferred_element_type=jnp.fl...  0.96 us
    dot_general x1, matrix products, body(): jnp.einsum('mk,kr->mr', deriv, full_third, preferred_element_type=jnp.flo...  0.92 us
  transfers between devices with their start and end apart: 14, of which 10 were waited for; matrix products, arithmetic and copies ran while one was open for 10% of the time, Pallas kernels for 0%

profile of v5, /device:TPU:0, one launch (start us, length us, event | category | flops | bytes accessed | tf_op | source)
XLA Modules:
  0.0 43.6 jit_solution(1904751140918552637)
XLA Ops:
  0.6 0.8 %reshape_reshape_reshape.28 = bf16[1024]{0:T(1024)(128)(2,1)S(1)} reshape(bf16[32,32]{1,0:T(8,128)(2,1)} %param.5) | data formatting | bytes 4096 | tf_op jit(solution)/shard_map/reshape;reshape;reshape | solution.py:26
  1.4 0.7 %pad_maximum_fusion.15 = bf16[3072]{0:T(1024)(128)(2,1)S(1)} fusion(bf16[2048]{0:T(1024)(128)(2,1)} %bitcast.233, bf16[1024]{0:T(1024)(128)(2,1)S(1)} %reshape_reshape_reshape.28), kind=kLoop, calls=%fused_computation.75 | loop fusion | flops 12288 | bytes 12288 | tf_op jit(solution)/shard_map/concatenate | solution.py:28
  2.1 5.0 %collective-permute-start.2 = (bf16[3072]{0:T(1024)(128)(2,1)S(1)}, bf16[3072]{0:T(1024)(128)(2,1)S(1)}, u32[]{:S(2)}, u32[]{:S(2)}) collective-permute-start(bf16[3072]{0:T(1024)(128)(2,1)S(1)} %pad_maximum_fusion.15), channel_id=1, source_target_pairs={{0,3},{1,2},{2,1},{3,0},{4,7},{5,6},{6,5},{7,4},{8,11},{9,10},{10,... | collective-permute-start | bytes 18440 | tf_op jit(solution)/shard_map/ppermute | solution.py:29
  7.2 0.6 %collective-permute-start = (bf16[3072]{0:T(1024)(128)(2,1)S(1)}, bf16[3072]{0:T(1024)(128)(2,1)S(1)}, u32[]{:S(2)}, u32[]{:S(2)}) collective-permute-start(bf16[3072]{0:T(1024)(128)(2,1)S(1)} %pad_maximum_fusion.15), channel_id=1, source_target_pairs={{0,1},{1,0},{2,3},{3,2},{4,5},{5,4},{6,7},{7,6},{8,9},{9,8},{10,11... | collective-permute-start | bytes 18440 | tf_op jit(solution)/shard_map/ppermute | solution.py:29
  7.7 0.8 %stack_reshape_reshape.15 = bf16[1,1,8,128]{3,2,1,0:T(8,128)(2,1)S(1)} reshape(bf16[32,32]{1,0:T(8,128)(2,1)} %param.5) | data formatting | bytes 4096 | tf_op jit(solution)/shard_map/stack;reshape;reshape | solution.py:61
  8.5 0.7 %copy.19 = bf16[4,2,8,128]{3,1,2,0:T(2,128)(2,1)S(1)} copy(bf16[4,2,8,128]{3,2,1,0:T(8,128)(2,1)} %bitcast.225) | data formatting | bytes 32768
  9.2 0.7 %stack_reshape_reshape.19 = bf16[1,1,64,128]{3,2,1,0:T(8,128)(2,1)S(1)} reshape(bf16[32,256]{1,0:T(8,128)(2,1)} %bitcast.226) | data formatting | bytes 32768 | tf_op jit(solution)/shard_map/stack;reshape;reshape | solution.py:61
  10.0 1.7 %collective-permute-done.1 = bf16[3072]{0:T(1024)(128)(2,1)S(1)} collective-permute-done((bf16[3072]{0:T(1024)(128)(2,1)S(1)}, bf16[3072]{0:T(1024)(128)(2,1)S(1)}, u32[]{:S(2)}, u32[]{:S(2)}) %collective-permute-start.1) | collective-permute-done | bytes 6176 | tf_op jit(solution)/shard_map/ppermute | solution.py:29
  11.9 0.7 %pad_maximum_fusion.10 = bf16[4,1,16,128]{3,2,1,0:T(8,128)(2,1)S(1)} fusion(bf16[1,1,16,128]{3,2,1,0:T(8,128)(2,1)S(1)} %slice_bitcast_fusion.24, bf16[1,1,16,128]{3,2,1,0:T(8,128)(2,1)S(1)} %slice_bitcast_fusion.25, bf16[1,1,16,128]{3,2,1,0:T(8,128)(2,1)S(1)} %slice_bitcast_fusion.26, bf16[1,1,16,128]{3,2,1,0:T(8,128)(2,1)} %bitcast.234), kind=kLoop, calls=%fused_computation.55 | loop fusion | flops 24576 | bytes 32768 | tf_op jit(solution)/shard_map/stack | solution.py:61
  13.1 1.6 %collective-permute-start.4 = (bf16[24576]{0:T(1024)(128)(2,1)S(1)}, bf16[24576]{0:T(1024)(128)(2,1)S(1)}, u32[]{:S(2)}, u32[]{:S(2)}) collective-permute-start(bf16[24576]{0:T(1024)(128)(2,1)S(1)} %pad_maximum_fusion.5), channel_id=1, source_target_pairs={{0,8},{8,0},{16,24},{24,16},{1,9},{9,1},{17,25},{25,17},{2,10},{10... | collective-permute-start | bytes 147464 | tf_op jit(solution)/shard_map/ppermute | solution.py:29
  14.6 1.5 %collective-permute-start.5 = (bf16[24576]{0:T(1024)(128)(2,1)S(1)}, bf16[24576]{0:T(1024)(128)(2,1)S(1)}, u32[]{:S(2)}, u32[]{:S(2)}) collective-permute-start(bf16[24576]{0:T(1024)(128)(2,1)S(1)} %pad_maximum_fusion.5), channel_id=1, source_target_pairs={{0,16},{8,24},{16,0},{24,8},{1,17},{9,25},{17,1},{25,9},{2,18},{10... | collective-permute-start | bytes 147464 | tf_op jit(solution)/shard_map/ppermute | solution.py:29
  16.1 0.5 %collective-permute-start.6 = (bf16[24576]{0:T(1024)(128)(2,1)S(1)}, bf16[24576]{0:T(1024)(128)(2,1)S(1)}, u32[]{:S(2)}, u32[]{:S(2)}) collective-permute-start(bf16[24576]{0:T(1024)(128)(2,1)S(1)} %pad_maximum_fusion.5), channel_id=1, source_target_pairs={{0,24},{8,16},{16,8},{24,0},{1,25},{9,17},{17,9},{25,1},{2,26},{10... | collective-permute-start | bytes 147464 | tf_op jit(solution)/shard_map/ppermute | solution.py:29
  17.2 1.5 %collective-permute-done.5 = bf16[24576]{0:T(1024)(128)(2,1)S(1)} collective-permute-done((bf16[24576]{0:T(1024)(128)(2,1)S(1)}, bf16[24576]{0:T(1024)(128)(2,1)S(1)}, u32[]{:S(2)}, u32[]{:S(2)}) %collective-permute-start.5) | collective-permute-done | bytes 49184 | tf_op jit(solution)/shard_map/ppermute | solution.py:29
  18.7 2.4 %collective-permute-done.6 = bf16[24576]{0:T(1024)(128)(2,1)S(1)} collective-permute-done((bf16[24576]{0:T(1024)(128)(2,1)S(1)}, bf16[24576]{0:T(1024)(128)(2,1)S(1)}, u32[]{:S(2)}, u32[]{:S(2)}) %collective-permute-start.6) | collective-permute-done | bytes 49184 | tf_op jit(solution)/shard_map/ppermute | solution.py:29
  21.6 0.6 %multiply_convert_fusion = bf16[32,128,256]{2,1,0:T(8,128)(2,1)S(1)} fusion(f32[128,256]{1,0:T(8,128)S(1)} %copy.15, f32[32,256]{1,0:T(8,128)S(1)} %reshape.292), kind=kLoop, calls=%fused_computation.5 | loop fusion | flops 2097152 | bytes 2260992 | tf_op jit(solution)/shard_map/convert_element_type | solution.py:97
  22.2 0.5 %copy-done = bf16[32,128,256]{2,1,0:T(8,128)(2,1)S(1)} copy-done((bf16[32,128,256]{2,1,0:T(8,128)(2,1)S(1)}, bf16[32,128,256]{2,1,0:T(8,128)(2,1)}, u32[]{:S(2)}) %copy-start) | copy-done | bytes 2097176
  22.8 0.9 %fusion.1 = bf16[4096,256]{1,0:T(8,128)(2,1)S(1)} fusion(bf16[32,128,256]{2,1,0:T(8,128)(2,1)S(1)} %copy-done, bf16[4096,256]{1,0:T(8,128)(2,1)S(1)} %bitcast.186, bf16[256,256]{1,0:T(8,128)(2,1)S(1)} %reshape_reshape_reshape.33), kind=kOutput, calls=%fused_computation.2 | convolution fusion | flops 541065216 | bytes 6422528 | tf_op jit(solution)/shard_map/mr,kr->mk/dot_general | solution.py:99
  23.6 1.0 %convolution_multiply_fusion = f32[256,256]{0,1:T(8,128)S(1)} fusion(bf16[4096,256]{1,0:T(8,128)(2,1)S(1)} %fusion.1, bf16[4096,256]{1,0:T(8,128)(2,1)S(1)} %bitcast.187), kind=kOutput, calls=%fused_computation.6 | convolution fusion | flops 536936448 | bytes 4456448 | tf_op jit(solution)/shard_map/mk,mr->kr/dot_general | solution.py:102
  24.6 0.9 %multiply_reduce_fusion.1 = (f32[32,256]{1,0:T(8,128)S(1)}, f32[128,256]{1,0:T(8,128)S(1)}) fusion(f32[128,256]{1,0:T(8,128)S(1)} %copy.15, f32[32,256]{1,0:T(8,128)S(1)} %reshape.292, bf16[32,128,256]{2,1,0:T(8,128)(2,1)S(1)} %bitcast.235, bf16[256,256,1]{1,0,2:T(8,128)(2,1)S(1)} %reshape.296), kind=kOutput, calls=%fused_computation.4 | convolution fusion | flops 541024256 | bytes 2555904 | tf_op jit(solution)/shard_map/mk,kr->mr/dot_general | solution.py:103
  25.8 0.6 %collective-permute-start.7 = (f32[24576]{0:T(1024)S(1)}, f32[24576]{0:T(1024)S(1)}, u32[]{:S(2)}, u32[]{:S(2)}) collective-permute-start(f32[24576]{0:T(1024)S(1)} %pad_maximum_fusion.1), channel_id=1, source_target_pairs={{0,8},{8,0},{16,24},{24,16},{1,9},{9,1},{17,25},{25,17},{2,10},{10... | collective-permute-start | bytes 294920 | tf_op jit(solution)/shard_map/ppermute | solution.py:29
  26.4 0.6 %collective-permute-start.8 = (f32[24576]{0:T(1024)S(1)}, f32[24576]{0:T(1024)S(1)}, u32[]{:S(2)}, u32[]{:S(2)}) collective-permute-start(f32[24576]{0:T(1024)S(1)} %pad_maximum_fusion.2), channel_id=1, source_target_pairs={{0,16},{8,24},{16,0},{24,8},{1,17},{9,25},{17,1},{25,9},{2,18},{10... | collective-permute-start | bytes 294920 | tf_op jit(solution)/shard_map/ppermute | solution.py:29
  27.0 2.5 %collective-permute-start.9 = (f32[24576]{0:T(1024)S(1)}, f32[24576]{0:T(1024)S(1)}, u32[]{:S(2)}, u32[]{:S(2)}) collective-permute-start(f32[24576]{0:T(1024)S(1)} %pad_maximum_fusion.3), channel_id=1, source_target_pairs={{0,24},{8,16},{16,8},{24,0},{1,25},{9,17},{17,9},{25,1},{2,26},{10... | collective-permute-start | bytes 294920 | tf_op jit(solution)/shard_map/ppermute | solution.py:29
  29.8 0.8 %collective-permute-done.7 = f32[24576]{0:T(1024)S(1)} collective-permute-done((f32[24576]{0:T(1024)S(1)}, f32[24576]{0:T(1024)S(1)}, u32[]{:S(2)}, u32[]{:S(2)}) %collective-permute-start.7) | collective-permute-done | bytes 98336 | tf_op jit(solution)/shard_map/ppermute | solution.py:29
  30.6 0.5 %collective-permute-done.8 = f32[24576]{0:T(1024)S(1)} collective-permute-done((f32[24576]{0:T(1024)S(1)}, f32[24576]{0:T(1024)S(1)}, u32[]{:S(2)}, u32[]{:S(2)}) %collective-permute-start.8) | collective-permute-done | bytes 98336 | tf_op jit(solution)/shard_map/ppermute | solution.py:29
  31.1 1.5 %collective-permute-done.9 = f32[24576]{0:T(1024)S(1)} collective-permute-done((f32[24576]{0:T(1024)S(1)}, f32[24576]{0:T(1024)S(1)}, u32[]{:S(2)}, u32[]{:S(2)}) %collective-permute-start.9) | collective-permute-done | bytes 98336 | tf_op jit(solution)/shard_map/ppermute | solution.py:29
  32.8 1.1 %collective-permute-done.10 = f32[12288]{0:T(1024)S(1)} collective-permute-done((f32[12288]{0:T(1024)S(1)}, f32[12288]{0:T(1024)S(1)}, u32[]{:S(2)}, u32[]{:S(2)}) %collective-permute-start.10) | collective-permute-done | bytes 49184 | tf_op jit(solution)/shard_map/ppermute | solution.py:29
  34.1 2.7 %collective-permute-start.12 = (f32[3072]{0:T(1024)S(1)}, f32[3072]{0:T(1024)S(1)}, u32[]{:S(2)}, u32[]{:S(2)}) collective-permute-start(f32[3072]{0:T(1024)S(1)} %pad_maximum_fusion.12), channel_id=1, source_target_pairs={{0,2},{1,3},{2,0},{3,1},{4,6},{5,7},{6,4},{7,5},{8,10},{9,11},{10,... | collective-permute-start | bytes 36872 | tf_op jit(solution)/shard_map/ppermute | solution.py:29
  36.8 1.6 %collective-permute-start.13 = (f32[3072]{0:T(1024)S(1)}, f32[3072]{0:T(1024)S(1)}, u32[]{:S(2)}, u32[]{:S(2)}) collective-permute-start(f32[3072]{0:T(1024)S(1)} %pad_maximum_fusion.13), channel_id=1, source_target_pairs={{0,3},{1,2},{2,1},{3,0},{4,7},{5,6},{6,5},{7,4},{8,11},{9,10},{10,... | collective-permute-start | bytes 36872 | tf_op jit(solution)/shard_map/ppermute | solution.py:29
  38.5 0.6 %reshape_squeeze.63 = f32[32,256]{1,0:T(8,128)} reshape(f32[64,128]{1,0:T(8,128)S(1)} %fusion.5) | data formatting | bytes 65536 | tf_op jit(solution)/shard_map/reshape;squeeze | solution.py:116
  39.1 3.2 %collective-permute-done.13 = f32[3072]{0:T(1024)S(1)} collective-permute-done((f32[3072]{0:T(1024)S(1)}, f32[3072]{0:T(1024)S(1)}, u32[]{:S(2)}, u32[]{:S(2)}) %collective-permute-start.13) | collective-permute-done | bytes 12320 | tf_op jit(solution)/shard_map/ppermute | solution.py:29
  42.3 0.7 %reshape_squeeze.62 = f32[32,32]{1,0:T(8,128)} reshape(f32[8,128]{1,0:T(8,128)S(1)} %fusion.15) | data formatting | bytes 8192 | tf_op jit(solution)/shard_map/reshape;squeeze | solution.py:114
  43.0 0.6 %fusion.12 = f32[128,16]{0,1:T(8,128)} fusion(f32[3072]{0:T(1024)S(1)} %collective-permute-done.13, f32[3072]{0:T(1024)S(1)} %collective-permute-done.12, f32[3072]{0:T(1024)S(1)} %collective-permute-done.11, f32[4,1,16,128]{3,2,1,0:T(8,128)S(1)} %bitcast.212), kind=kLoop, calls=%fused_computation.64 | loop fusion | flops 6144 | bytes 40960 | tf_op jit(solution)/shard_map/transpose | solution.py:115
  (91 shorter events, 2.3 us)
Async XLA Ops:
  2.1 7.9 %collective-permute-start.2 = (bf16[3072]{0:T(1024)(128)(2,1)S(1)}, bf16[3072]{0:T(1024)(128)(2,1)S(1)}, u32[]{:S(2)}, u32[]{:S(2)}) collective-permute-start(bf16[3072]{0:T(1024)(128)(2,1)S(1)} %pad_maximum_fusion.15), channel_id=1, source_target_pairs={{0,3},{1,2},{2,1},{3,0},{4,7},{5,6},{6,5},{7,4},{8,11},{9,10},{10,... | collective-permute-start | bytes 18440 | tf_op jit(solution)/shard_map/ppermute | solution.py:29
  7.2 4.5 %collective-permute-start.1 = (bf16[3072]{0:T(1024)(128)(2,1)S(1)}, bf16[3072]{0:T(1024)(128)(2,1)S(1)}, u32[]{:S(2)}, u32[]{:S(2)}) collective-permute-start(bf16[3072]{0:T(1024)(128)(2,1)S(1)} %pad_maximum_fusion.15), channel_id=1, source_target_pairs={{0,2},{1,3},{2,0},{3,1},{4,6},{5,7},{6,4},{7,5},{8,10},{9,11},{10,... | collective-permute-start | bytes 18440 | tf_op jit(solution)/shard_map/ppermute | solution.py:29
  7.2 4.5 %collective-permute-start = (bf16[3072]{0:T(1024)(128)(2,1)S(1)}, bf16[3072]{0:T(1024)(128)(2,1)S(1)}, u32[]{:S(2)}, u32[]{:S(2)}) collective-permute-start(bf16[3072]{0:T(1024)(128)(2,1)S(1)} %pad_maximum_fusion.15), channel_id=1, source_target_pairs={{0,1},{1,0},{2,3},{3,2},{4,5},{5,4},{6,7},{7,6},{8,9},{9,8},{10,11... | collective-permute-start | bytes 18440 | tf_op jit(solution)/shard_map/ppermute | solution.py:29
  11.7 1.3 %collective-permute-start.3 = (bf16[12288]{0:T(1024)(128)(2,1)S(1)}, bf16[12288]{0:T(1024)(128)(2,1)S(1)}, u32[]{:S(2)}, u32[]{:S(2)}) collective-permute-start(bf16[12288]{0:T(1024)(128)(2,1)S(1)} %pad_maximum_fusion.8), channel_id=1, source_target_pairs={{0,4},{4,0},{1,5},{5,1},{2,6},{6,2},{3,7},{7,3},{8,12},{12,8},{9,1... | collective-permute-start | bytes 73736 | tf_op jit(solution)/shard_map/ppermute | solution.py:29
  13.1 4.2 %collective-permute-start.4 = (bf16[24576]{0:T(1024)(128)(2,1)S(1)}, bf16[24576]{0:T(1024)(128)(2,1)S(1)}, u32[]{:S(2)}, u32[]{:S(2)}) collective-permute-start(bf16[24576]{0:T(1024)(128)(2,1)S(1)} %pad_maximum_fusion.5), channel_id=1, source_target_pairs={{0,8},{8,0},{16,24},{24,16},{1,9},{9,1},{17,25},{25,17},{2,10},{10... | collective-permute-start | bytes 147464 | tf_op jit(solution)/shard_map/ppermute | solution.py:29
  14.6 4.1 %collective-permute-start.5 = (bf16[24576]{0:T(1024)(128)(2,1)S(1)}, bf16[24576]{0:T(1024)(128)(2,1)S(1)}, u32[]{:S(2)}, u32[]{:S(2)}) collective-permute-start(bf16[24576]{0:T(1024)(128)(2,1)S(1)} %pad_maximum_fusion.5), channel_id=1, source_target_pairs={{0,16},{8,24},{16,0},{24,8},{1,17},{9,25},{17,1},{25,9},{2,18},{10... | collective-permute-start | bytes 147464 | tf_op jit(solution)/shard_map/ppermute | solution.py:29
  16.1 5.0 %collective-permute-start.6 = (bf16[24576]{0:T(1024)(128)(2,1)S(1)}, bf16[24576]{0:T(1024)(128)(2,1)S(1)}, u32[]{:S(2)}, u32[]{:S(2)}) collective-permute-start(bf16[24576]{0:T(1024)(128)(2,1)S(1)} %pad_maximum_fusion.5), channel_id=1, source_target_pairs={{0,24},{8,16},{16,8},{24,0},{1,25},{9,17},{17,9},{25,1},{2,26},{10... | collective-permute-start | bytes 147464 | tf_op jit(solution)/shard_map/ppermute | solution.py:29
  21.2 1.6 %copy-start = (bf16[32,128,256]{2,1,0:T(8,128)(2,1)S(1)}, bf16[32,128,256]{2,1,0:T(8,128)(2,1)}, u32[]{:S(2)}) copy-start(bf16[32,128,256]{2,1,0:T(8,128)(2,1)} %param.4) | copy-start | bytes 6291460
  25.8 4.8 %collective-permute-start.7 = (f32[24576]{0:T(1024)S(1)}, f32[24576]{0:T(1024)S(1)}, u32[]{:S(2)}, u32[]{:S(2)}) collective-permute-start(f32[24576]{0:T(1024)S(1)} %pad_maximum_fusion.1), channel_id=1, source_target_pairs={{0,8},{8,0},{16,24},{24,16},{1,9},{9,1},{17,25},{25,17},{2,10},{10... | collective-permute-start | bytes 294920 | tf_op jit(solution)/shard_map/ppermute | solution.py:29
  26.4 4.7 %collective-permute-start.8 = (f32[24576]{0:T(1024)S(1)}, f32[24576]{0:T(1024)S(1)}, u32[]{:S(2)}, u32[]{:S(2)}) collective-permute-start(f32[24576]{0:T(1024)S(1)} %pad_maximum_fusion.2), channel_id=1, source_target_pairs={{0,16},{8,24},{16,0},{24,8},{1,17},{9,25},{17,1},{25,9},{2,18},{10... | collective-permute-start | bytes 294920 | tf_op jit(solution)/shard_map/ppermute | solution.py:29
  27.0 5.6 %collective-permute-start.9 = (f32[24576]{0:T(1024)S(1)}, f32[24576]{0:T(1024)S(1)}, u32[]{:S(2)}, u32[]{:S(2)}) collective-permute-start(f32[24576]{0:T(1024)S(1)} %pad_maximum_fusion.3), channel_id=1, source_target_pairs={{0,24},{8,16},{16,8},{24,0},{1,25},{9,17},{17,9},{25,1},{2,26},{10... | collective-permute-start | bytes 294920 | tf_op jit(solution)/shard_map/ppermute | solution.py:29
  32.7 1.3 %collective-permute-start.10 = (f32[12288]{0:T(1024)S(1)}, f32[12288]{0:T(1024)S(1)}, u32[]{:S(2)}, u32[]{:S(2)}) collective-permute-start(f32[12288]{0:T(1024)S(1)} %pad_maximum_fusion.6), channel_id=1, source_target_pairs={{0,4},{4,0},{1,5},{5,1},{2,6},{6,2},{3,7},{7,3},{8,12},{12,8},{9,1... | collective-permute-start | bytes 147464 | tf_op jit(solution)/shard_map/ppermute | solution.py:29
  34.0 5.1 %collective-permute-start.11 = (f32[3072]{0:T(1024)S(1)}, f32[3072]{0:T(1024)S(1)}, u32[]{:S(2)}, u32[]{:S(2)}) collective-permute-start(f32[3072]{0:T(1024)S(1)} %pad_maximum_fusion.11), channel_id=1, source_target_pairs={{0,1},{1,0},{2,3},{3,2},{4,5},{5,4},{6,7},{7,6},{8,9},{9,8},{10,11... | collective-permute-start | bytes 36872 | tf_op jit(solution)/shard_map/ppermute | solution.py:29
  34.1 5.0 %collective-permute-start.12 = (f32[3072]{0:T(1024)S(1)}, f32[3072]{0:T(1024)S(1)}, u32[]{:S(2)}, u32[]{:S(2)}) collective-permute-start(f32[3072]{0:T(1024)S(1)} %pad_maximum_fusion.12), channel_id=1, source_target_pairs={{0,2},{1,3},{2,0},{3,1},{4,6},{5,7},{6,4},{7,5},{8,10},{9,11},{10,... | collective-permute-start | bytes 36872 | tf_op jit(solution)/shard_map/ppermute | solution.py:29
  36.8 5.5 %collective-permute-start.13 = (f32[3072]{0:T(1024)S(1)}, f32[3072]{0:T(1024)S(1)}, u32[]{:S(2)}, u32[]{:S(2)}) collective-permute-start(f32[3072]{0:T(1024)S(1)} %pad_maximum_fusion.13), channel_id=1, source_target_pairs={{0,3},{1,2},{2,1},{3,0},{4,7},{5,6},{6,5},{7,4},{8,11},{9,10},{10,... | collective-permute-start | bytes 36872 | tf_op jit(solution)/shard_map/ppermute | solution.py:29

commit v6 on v5

--- a/solution.py
+++ b/solution.py
@@ -55,7 +55,8 @@
         for t, r in _digits(lax.axis_size(axis)):
             who = [f for f, g in enumerate(GROUPS) if axis in g]
             mine = [accs[f] for f in who]
-            got = [_exchange(mine, axis, t, s) for s in range(1, r)]
+            got = {s: _exchange(mine, axis, t, s) for s in range(r - 1, 0, -1)}
+            got = [got[s] for s in range(1, r)]
             d = _digit(axis, t, r)
             for i, f in enumerate(who):
                 cands = _flip_by(jnp.stack([mine[i]] + [g[i] for g in got]), d, r)
@@ -72,7 +73,7 @@
             subs = [_flip_by(accs[f].reshape((r, accs[f].shape[0] // r) + accs[f].shape[1:]), d, r) for f in who]
             for f, sub in zip(who, subs):
                 accs[f] = sub[0]
-            for s in range(1, r):
+            for s in range(r - 1, 0, -1):
                 got = _exchange([sub[s] for sub in subs], axis, t, s)
                 for f, g in zip(who, got):
                     accs[f] = accs[f] + g

time: 44.1 us -> 42.7 us (0.968)
  waiting for transfers between devices: 13.5 us -> 12.1 us
    ppermute x14, waiting for transfers between devices: 13.5 us -> 12.1 us  [_exchange(): got = lax.ppermute(payload, axis, [(i, i ^ s << t) for i in range(n)])]
  transfers between devices with their start and end apart: 14 -> 14, of which waited for: 10 -> 11; matrix products, arithmetic and copies ran while one was open for 10% -> 10% of each run, Pallas kernels for 0% -> 0%
where the time goes in v6:
time: 42.7 us; the launch traced here: 42.2 us
  starting transfers between devices  17.4 us (41%)
  waiting for transfers between devices  12.1 us (28%)
  local copies, waits for them, and re-layouts  5.72 us (13%)
  other arithmetic  3.09 us (7%)
  matrix products  2.75 us (6%)
  between operations  1.16 us (3%)
    ppermute x14, starting transfers between devices, _exchange(): got = lax.ppermute(payload, axis, [(i, i ^ s << t) for i in range(n)])  17.4 us
    ppermute x14, waiting for transfers between devices, _exchange(): got = lax.ppermute(payload, axis, [(i, i ^ s << t) for i in range(n)])  12.1 us
    another operation x6, local copies, waits for them, and re-layouts, gather_all(): cands = _flip_by(jnp.stack([mine[i]] + [g[i] for g in got]), d, r)  1.52 us
    unnamed x3, local copies, waits for them, and re-layouts  1.26 us
    dot_general x1, matrix products, body(): jnp.einsum('mk,mr->kr', deriv, khatri_flat, preferred_element_type=jnp.fl...  0.96 us
    dot_general x1, matrix products, body(): jnp.einsum('mk,kr->mr', deriv, full_third, preferred_element_type=jnp.flo...  0.92 us
    dot_general x1, matrix products, body(): jnp.einsum('mr,kr->mk', khatri_flat, full_third, preferred_element_type=j...  0.87 us
  transfers between devices with their start and end apart: 14, of which 11 were waited for; matrix products, arithmetic and copies ran while one was open for 10% of the time, Pallas kernels for 0%

profile of v6, /device:TPU:0, one launch (start us, length us, event | category | flops | bytes accessed | tf_op | source)
XLA Modules:
  0.0 42.2 jit_solution(6370443716260045978)
XLA Ops:
  0.6 0.8 %reshape_reshape_reshape.28 = bf16[1024]{0:T(1024)(128)(2,1)S(1)} reshape(bf16[32,32]{1,0:T(8,128)(2,1)} %param.5) | data formatting | bytes 4096 | tf_op jit(solution)/shard_map/reshape;reshape;reshape | solution.py:26
  1.4 0.7 %pad_maximum_fusion.15 = bf16[3072]{0:T(1024)(128)(2,1)S(1)} fusion(bf16[2048]{0:T(1024)(128)(2,1)} %bitcast.233, bf16[1024]{0:T(1024)(128)(2,1)S(1)} %reshape_reshape_reshape.28), kind=kLoop, calls=%fused_computation.75 | loop fusion | flops 12288 | bytes 12288 | tf_op jit(solution)/shard_map/concatenate | solution.py:28
  2.1 5.0 %collective-permute-start.2 = (bf16[3072]{0:T(1024)(128)(2,1)S(1)}, bf16[3072]{0:T(1024)(128)(2,1)S(1)}, u32[]{:S(2)}, u32[]{:S(2)}) collective-permute-start(bf16[3072]{0:T(1024)(128)(2,1)S(1)} %pad_maximum_fusion.15), channel_id=1, source_target_pairs={{0,3},{1,2},{2,1},{3,0},{4,7},{5,6},{6,5},{7,4},{8,11},{9,10},{10,... | collective-permute-start | bytes 18440 | tf_op jit(solution)/shard_map/ppermute | solution.py:29
  7.2 0.6 %collective-permute-start = (bf16[3072]{0:T(1024)(128)(2,1)S(1)}, bf16[3072]{0:T(1024)(128)(2,1)S(1)}, u32[]{:S(2)}, u32[]{:S(2)}) collective-permute-start(bf16[3072]{0:T(1024)(128)(2,1)S(1)} %pad_maximum_fusion.15), channel_id=1, source_target_pairs={{0,1},{1,0},{2,3},{3,2},{4,5},{5,4},{6,7},{7,6},{8,9},{9,8},{10,11... | collective-permute-start | bytes 18440 | tf_op jit(solution)/shard_map/ppermute | solution.py:29
  7.7 0.8 %stack_reshape_reshape.15 = bf16[1,1,8,128]{3,2,1,0:T(8,128)(2,1)S(1)} reshape(bf16[32,32]{1,0:T(8,128)(2,1)} %param.5) | data formatting | bytes 4096 | tf_op jit(solution)/shard_map/stack;reshape;reshape | solution.py:62
  8.5 0.7 %copy.19 = bf16[4,2,8,128]{3,1,2,0:T(2,128)(2,1)S(1)} copy(bf16[4,2,8,128]{3,2,1,0:T(8,128)(2,1)} %bitcast.225) | data formatting | bytes 32768
  9.2 0.7 %stack_reshape_reshape.19 = bf16[1,1,64,128]{3,2,1,0:T(8,128)(2,1)S(1)} reshape(bf16[32,256]{1,0:T(8,128)(2,1)} %bitcast.226) | data formatting | bytes 32768 | tf_op jit(solution)/shard_map/stack;reshape;reshape | solution.py:62
  10.0 1.7 %collective-permute-done.1 = bf16[3072]{0:T(1024)(128)(2,1)S(1)} collective-permute-done((bf16[3072]{0:T(1024)(128)(2,1)S(1)}, bf16[3072]{0:T(1024)(128)(2,1)S(1)}, u32[]{:S(2)}, u32[]{:S(2)}) %collective-permute-start.1) | collective-permute-done | bytes 6176 | tf_op jit(solution)/shard_map/ppermute | solution.py:29
  11.9 0.7 %pad_maximum_fusion.10 = bf16[4,1,16,128]{3,2,1,0:T(8,128)(2,1)S(1)} fusion(bf16[1,1,16,128]{3,2,1,0:T(8,128)(2,1)S(1)} %slice_bitcast_fusion.24, bf16[1,1,16,128]{3,2,1,0:T(8,128)(2,1)S(1)} %slice_bitcast_fusion.25, bf16[1,1,16,128]{3,2,1,0:T(8,128)(2,1)S(1)} %slice_bitcast_fusion.26, bf16[1,1,16,128]{3,2,1,0:T(8,128)(2,1)} %bitcast.234), kind=kLoop, calls=%fused_computation.55 | loop fusion | flops 24576 | bytes 32768 | tf_op jit(solution)/shard_map/stack | solution.py:62
  13.1 1.6 %collective-permute-start.4 = (bf16[24576]{0:T(1024)(128)(2,1)S(1)}, bf16[24576]{0:T(1024)(128)(2,1)S(1)}, u32[]{:S(2)}, u32[]{:S(2)}) collective-permute-start(bf16[24576]{0:T(1024)(128)(2,1)S(1)} %pad_maximum_fusion.5), channel_id=1, source_target_pairs={{0,8},{8,0},{16,24},{24,16},{1,9},{9,1},{17,25},{25,17},{2,10},{10... | collective-permute-start | bytes 147464 | tf_op jit(solution)/shard_map/ppermute | solution.py:29
  14.6 1.5 %collective-permute-start.5 = (bf16[24576]{0:T(1024)(128)(2,1)S(1)}, bf16[24576]{0:T(1024)(128)(2,1)S(1)}, u32[]{:S(2)}, u32[]{:S(2)}) collective-permute-start(bf16[24576]{0:T(1024)(128)(2,1)S(1)} %pad_maximum_fusion.5), channel_id=1, source_target_pairs={{0,16},{8,24},{16,0},{24,8},{1,17},{9,25},{17,1},{25,9},{2,18},{10... | collective-permute-start | bytes 147464 | tf_op jit(solution)/shard_map/ppermute | solution.py:29
  17.2 1.5 %collective-permute-done.5 = bf16[24576]{0:T(1024)(128)(2,1)S(1)} collective-permute-done((bf16[24576]{0:T(1024)(128)(2,1)S(1)}, bf16[24576]{0:T(1024)(128)(2,1)S(1)}, u32[]{:S(2)}, u32[]{:S(2)}) %collective-permute-start.5) | collective-permute-done | bytes 49184 | tf_op jit(solution)/shard_map/ppermute | solution.py:29
  18.7 2.4 %collective-permute-done.6 = bf16[24576]{0:T(1024)(128)(2,1)S(1)} collective-permute-done((bf16[24576]{0:T(1024)(128)(2,1)S(1)}, bf16[24576]{0:T(1024)(128)(2,1)S(1)}, u32[]{:S(2)}, u32[]{:S(2)}) %collective-permute-start.6) | collective-permute-done | bytes 49184 | tf_op jit(solution)/shard_map/ppermute | solution.py:29
  21.6 0.6 %multiply_convert_fusion = bf16[32,128,256]{2,1,0:T(8,128)(2,1)S(1)} fusion(f32[128,256]{1,0:T(8,128)S(1)} %copy.15, f32[32,256]{1,0:T(8,128)S(1)} %reshape.292), kind=kLoop, calls=%fused_computation.5 | loop fusion | flops 2097152 | bytes 2260992 | tf_op jit(solution)/shard_map/convert_element_type | solution.py:98
  22.2 0.5 %copy-done = bf16[32,128,256]{2,1,0:T(8,128)(2,1)S(1)} copy-done((bf16[32,128,256]{2,1,0:T(8,128)(2,1)S(1)}, bf16[32,128,256]{2,1,0:T(8,128)(2,1)}, u32[]{:S(2)}) %copy-start) | copy-done | bytes 2097176
  22.8 0.9 %fusion.1 = bf16[4096,256]{1,0:T(8,128)(2,1)S(1)} fusion(bf16[32,128,256]{2,1,0:T(8,128)(2,1)S(1)} %copy-done, bf16[4096,256]{1,0:T(8,128)(2,1)S(1)} %bitcast.186, bf16[256,256]{1,0:T(8,128)(2,1)S(1)} %reshape_reshape_reshape.33), kind=kOutput, calls=%fused_computation.2 | convolution fusion | flops 541065216 | bytes 6422528 | tf_op jit(solution)/shard_map/mr,kr->mk/dot_general | solution.py:100
  23.6 1.0 %convolution_multiply_fusion = f32[256,256]{0,1:T(8,128)S(1)} fusion(bf16[4096,256]{1,0:T(8,128)(2,1)S(1)} %fusion.1, bf16[4096,256]{1,0:T(8,128)(2,1)S(1)} %bitcast.187), kind=kOutput, calls=%fused_computation.6 | convolution fusion | flops 536936448 | bytes 4456448 | tf_op jit(solution)/shard_map/mk,mr->kr/dot_general | solution.py:103
  24.6 0.9 %multiply_reduce_fusion.1 = (f32[32,256]{1,0:T(8,128)S(1)}, f32[128,256]{1,0:T(8,128)S(1)}) fusion(f32[128,256]{1,0:T(8,128)S(1)} %copy.15, f32[32,256]{1,0:T(8,128)S(1)} %reshape.292, bf16[32,128,256]{2,1,0:T(8,128)(2,1)S(1)} %bitcast.235, bf16[256,256,1]{1,0,2:T(8,128)(2,1)S(1)} %reshape.296), kind=kOutput, calls=%fused_computation.4 | convolution fusion | flops 541024256 | bytes 2555904 | tf_op jit(solution)/shard_map/mk,kr->mr/dot_general | solution.py:104
  25.8 0.5 %collective-permute-start.7 = (f32[24576]{0:T(1024)S(1)}, f32[24576]{0:T(1024)S(1)}, u32[]{:S(2)}, u32[]{:S(2)}) collective-permute-start(f32[24576]{0:T(1024)S(1)} %pad_maximum_fusion.1), channel_id=1, source_target_pairs={{0,24},{8,16},{16,8},{24,0},{1,25},{9,17},{17,9},{25,1},{2,26},{10... | collective-permute-start | bytes 294920 | tf_op jit(solution)/shard_map/ppermute | solution.py:29
  26.4 1.6 %collective-permute-start.8 = (f32[24576]{0:T(1024)S(1)}, f32[24576]{0:T(1024)S(1)}, u32[]{:S(2)}, u32[]{:S(2)}) collective-permute-start(f32[24576]{0:T(1024)S(1)} %pad_maximum_fusion.2), channel_id=1, source_target_pairs={{0,16},{8,24},{16,0},{24,8},{1,17},{9,25},{17,1},{25,9},{2,18},{10... | collective-permute-start | bytes 294920 | tf_op jit(solution)/shard_map/ppermute | solution.py:29
  28.0 1.6 %collective-permute-start.9 = (f32[24576]{0:T(1024)S(1)}, f32[24576]{0:T(1024)S(1)}, u32[]{:S(2)}, u32[]{:S(2)}) collective-permute-start(f32[24576]{0:T(1024)S(1)} %pad_maximum_fusion.3), channel_id=1, source_target_pairs={{0,8},{8,0},{16,24},{24,16},{1,9},{9,1},{17,25},{25,17},{2,10},{10... | collective-permute-start | bytes 294920 | tf_op jit(solution)/shard_map/ppermute | solution.py:29
  29.8 1.7 %collective-permute-done.7 = f32[24576]{0:T(1024)S(1)} collective-permute-done((f32[24576]{0:T(1024)S(1)}, f32[24576]{0:T(1024)S(1)}, u32[]{:S(2)}, u32[]{:S(2)}) %collective-permute-start.7) | collective-permute-done | bytes 98336 | tf_op jit(solution)/shard_map/ppermute | solution.py:29
  31.5 0.6 %collective-permute-done.8 = f32[24576]{0:T(1024)S(1)} collective-permute-done((f32[24576]{0:T(1024)S(1)}, f32[24576]{0:T(1024)S(1)}, u32[]{:S(2)}, u32[]{:S(2)}) %collective-permute-start.8) | collective-permute-done | bytes 98336 | tf_op jit(solution)/shard_map/ppermute | solution.py:29
  32.1 0.5 %collective-permute-done.9 = f32[24576]{0:T(1024)S(1)} collective-permute-done((f32[24576]{0:T(1024)S(1)}, f32[24576]{0:T(1024)S(1)}, u32[]{:S(2)}, u32[]{:S(2)}) %collective-permute-start.9) | collective-permute-done | bytes 98336 | tf_op jit(solution)/shard_map/ppermute | solution.py:29
  32.9 1.1 %collective-permute-done.10 = f32[12288]{0:T(1024)S(1)} collective-permute-done((f32[12288]{0:T(1024)S(1)}, f32[12288]{0:T(1024)S(1)}, u32[]{:S(2)}, u32[]{:S(2)}) %collective-permute-start.10) | collective-permute-done | bytes 49184 | tf_op jit(solution)/shard_map/ppermute | solution.py:29
  34.1 2.3 %collective-permute-start.11 = (f32[3072]{0:T(1024)S(1)}, f32[3072]{0:T(1024)S(1)}, u32[]{:S(2)}, u32[]{:S(2)}) collective-permute-start(f32[3072]{0:T(1024)S(1)} %pad_maximum_fusion.11), channel_id=1, source_target_pairs={{0,3},{1,2},{2,1},{3,0},{4,7},{5,6},{6,5},{7,4},{8,11},{9,10},{10,... | collective-permute-start | bytes 36872 | tf_op jit(solution)/shard_map/ppermute | solution.py:29
  36.3 2.2 %collective-permute-start.13 = (f32[3072]{0:T(1024)S(1)}, f32[3072]{0:T(1024)S(1)}, u32[]{:S(2)}, u32[]{:S(2)}) collective-permute-start(f32[3072]{0:T(1024)S(1)} %pad_maximum_fusion.13), channel_id=1, source_target_pairs={{0,1},{1,0},{2,3},{3,2},{4,5},{5,4},{6,7},{7,6},{8,9},{9,8},{10,11... | collective-permute-start | bytes 36872 | tf_op jit(solution)/shard_map/ppermute | solution.py:29
  38.5 0.6 %reshape_squeeze.63 = f32[32,256]{1,0:T(8,128)} reshape(f32[64,128]{1,0:T(8,128)S(1)} %fusion.5) | data formatting | bytes 65536 | tf_op jit(solution)/shard_map/reshape;squeeze | solution.py:117
  39.1 0.6 %collective-permute-done.11 = f32[3072]{0:T(1024)S(1)} collective-permute-done((f32[3072]{0:T(1024)S(1)}, f32[3072]{0:T(1024)S(1)}, u32[]{:S(2)}, u32[]{:S(2)}) %collective-permute-start.11) | collective-permute-done | bytes 12320 | tf_op jit(solution)/shard_map/ppermute | solution.py:29
  39.7 1.2 %collective-permute-done.12 = f32[3072]{0:T(1024)S(1)} collective-permute-done((f32[3072]{0:T(1024)S(1)}, f32[3072]{0:T(1024)S(1)}, u32[]{:S(2)}, u32[]{:S(2)}) %collective-permute-start.12) | collective-permute-done | bytes 12320 | tf_op jit(solution)/shard_map/ppermute | solution.py:29
  40.9 0.7 %reshape_squeeze.62 = f32[32,32]{1,0:T(8,128)} reshape(f32[8,128]{1,0:T(8,128)S(1)} %fusion.15) | data formatting | bytes 8192 | tf_op jit(solution)/shard_map/reshape;squeeze | solution.py:115
  41.6 0.6 %fusion.12 = f32[128,16]{0,1:T(8,128)} fusion(f32[3072]{0:T(1024)S(1)} %collective-permute-done.13, f32[3072]{0:T(1024)S(1)} %collective-permute-done.12, f32[3072]{0:T(1024)S(1)} %collective-permute-done.11, f32[4,1,16,128]{3,2,1,0:T(8,128)S(1)} %bitcast.212), kind=kLoop, calls=%fused_computation.64 | loop fusion | flops 6144 | bytes 40960 | tf_op jit(solution)/shard_map/transpose | solution.py:116
  (91 shorter events, 2.7 us)
Async XLA Ops:
  2.1 7.9 %collective-permute-start.2 = (bf16[3072]{0:T(1024)(128)(2,1)S(1)}, bf16[3072]{0:T(1024)(128)(2,1)S(1)}, u32[]{:S(2)}, u32[]{:S(2)}) collective-permute-start(bf16[3072]{0:T(1024)(128)(2,1)S(1)} %pad_maximum_fusion.15), channel_id=1, source_target_pairs={{0,3},{1,2},{2,1},{3,0},{4,7},{5,6},{6,5},{7,4},{8,11},{9,10},{10,... | collective-permute-start | bytes 18440 | tf_op jit(solution)/shard_map/ppermute | solution.py:29
  7.2 4.5 %collective-permute-start.1 = (bf16[3072]{0:T(1024)(128)(2,1)S(1)}, bf16[3072]{0:T(1024)(128)(2,1)S(1)}, u32[]{:S(2)}, u32[]{:S(2)}) collective-permute-start(bf16[3072]{0:T(1024)(128)(2,1)S(1)} %pad_maximum_fusion.15), channel_id=1, source_target_pairs={{0,2},{1,3},{2,0},{3,1},{4,6},{5,7},{6,4},{7,5},{8,10},{9,11},{10,... | collective-permute-start | bytes 18440 | tf_op jit(solution)/shard_map/ppermute | solution.py:29
  7.2 4.5 %collective-permute-start = (bf16[3072]{0:T(1024)(128)(2,1)S(1)}, bf16[3072]{0:T(1024)(128)(2,1)S(1)}, u32[]{:S(2)}, u32[]{:S(2)}) collective-permute-start(bf16[3072]{0:T(1024)(128)(2,1)S(1)} %pad_maximum_fusion.15), channel_id=1, source_target_pairs={{0,1},{1,0},{2,3},{3,2},{4,5},{5,4},{6,7},{7,6},{8,9},{9,8},{10,11... | collective-permute-start | bytes 18440 | tf_op jit(solution)/shard_map/ppermute | solution.py:29
  11.7 1.3 %collective-permute-start.3 = (bf16[12288]{0:T(1024)(128)(2,1)S(1)}, bf16[12288]{0:T(1024)(128)(2,1)S(1)}, u32[]{:S(2)}, u32[]{:S(2)}) collective-permute-start(bf16[12288]{0:T(1024)(128)(2,1)S(1)} %pad_maximum_fusion.8), channel_id=1, source_target_pairs={{0,4},{4,0},{1,5},{5,1},{2,6},{6,2},{3,7},{7,3},{8,12},{12,8},{9,1... | collective-permute-start | bytes 73736 | tf_op jit(solution)/shard_map/ppermute | solution.py:29
  13.1 4.2 %collective-permute-start.4 = (bf16[24576]{0:T(1024)(128)(2,1)S(1)}, bf16[24576]{0:T(1024)(128)(2,1)S(1)}, u32[]{:S(2)}, u32[]{:S(2)}) collective-permute-start(bf16[24576]{0:T(1024)(128)(2,1)S(1)} %pad_maximum_fusion.5), channel_id=1, source_target_pairs={{0,8},{8,0},{16,24},{24,16},{1,9},{9,1},{17,25},{25,17},{2,10},{10... | collective-permute-start | bytes 147464 | tf_op jit(solution)/shard_map/ppermute | solution.py:29
  14.6 4.1 %collective-permute-start.5 = (bf16[24576]{0:T(1024)(128)(2,1)S(1)}, bf16[24576]{0:T(1024)(128)(2,1)S(1)}, u32[]{:S(2)}, u32[]{:S(2)}) collective-permute-start(bf16[24576]{0:T(1024)(128)(2,1)S(1)} %pad_maximum_fusion.5), channel_id=1, source_target_pairs={{0,16},{8,24},{16,0},{24,8},{1,17},{9,25},{17,1},{25,9},{2,18},{10... | collective-permute-start | bytes 147464 | tf_op jit(solution)/shard_map/ppermute | solution.py:29
  16.1 5.0 %collective-permute-start.6 = (bf16[24576]{0:T(1024)(128)(2,1)S(1)}, bf16[24576]{0:T(1024)(128)(2,1)S(1)}, u32[]{:S(2)}, u32[]{:S(2)}) collective-permute-start(bf16[24576]{0:T(1024)(128)(2,1)S(1)} %pad_maximum_fusion.5), channel_id=1, source_target_pairs={{0,24},{8,16},{16,8},{24,0},{1,25},{9,17},{17,9},{25,1},{2,26},{10... | collective-permute-start | bytes 147464 | tf_op jit(solution)/shard_map/ppermute | solution.py:29
  21.2 1.6 %copy-start = (bf16[32,128,256]{2,1,0:T(8,128)(2,1)S(1)}, bf16[32,128,256]{2,1,0:T(8,128)(2,1)}, u32[]{:S(2)}) copy-start(bf16[32,128,256]{2,1,0:T(8,128)(2,1)} %param.4) | copy-start | bytes 6291460
  25.8 5.7 %collective-permute-start.7 = (f32[24576]{0:T(1024)S(1)}, f32[24576]{0:T(1024)S(1)}, u32[]{:S(2)}, u32[]{:S(2)}) collective-permute-start(f32[24576]{0:T(1024)S(1)} %pad_maximum_fusion.1), channel_id=1, source_target_pairs={{0,24},{8,16},{16,8},{24,0},{1,25},{9,17},{17,9},{25,1},{2,26},{10... | collective-permute-start | bytes 294920 | tf_op jit(solution)/shard_map/ppermute | solution.py:29
  26.4 5.7 %collective-permute-start.8 = (f32[24576]{0:T(1024)S(1)}, f32[24576]{0:T(1024)S(1)}, u32[]{:S(2)}, u32[]{:S(2)}) collective-permute-start(f32[24576]{0:T(1024)S(1)} %pad_maximum_fusion.2), channel_id=1, source_target_pairs={{0,16},{8,24},{16,0},{24,8},{1,17},{9,25},{17,1},{25,9},{2,18},{10... | collective-permute-start | bytes 294920 | tf_op jit(solution)/shard_map/ppermute | solution.py:29
  28.0 4.7 %collective-permute-start.9 = (f32[24576]{0:T(1024)S(1)}, f32[24576]{0:T(1024)S(1)}, u32[]{:S(2)}, u32[]{:S(2)}) collective-permute-start(f32[24576]{0:T(1024)S(1)} %pad_maximum_fusion.3), channel_id=1, source_target_pairs={{0,8},{8,0},{16,24},{24,16},{1,9},{9,1},{17,25},{25,17},{2,10},{10... | collective-permute-start | bytes 294920 | tf_op jit(solution)/shard_map/ppermute | solution.py:29
  32.7 1.3 %collective-permute-start.10 = (f32[12288]{0:T(1024)S(1)}, f32[12288]{0:T(1024)S(1)}, u32[]{:S(2)}, u32[]{:S(2)}) collective-permute-start(f32[12288]{0:T(1024)S(1)} %pad_maximum_fusion.6), channel_id=1, source_target_pairs={{0,4},{4,0},{1,5},{5,1},{2,6},{6,2},{3,7},{7,3},{8,12},{12,8},{9,1... | collective-permute-start | bytes 147464 | tf_op jit(solution)/shard_map/ppermute | solution.py:29
  34.1 5.7 %collective-permute-start.11 = (f32[3072]{0:T(1024)S(1)}, f32[3072]{0:T(1024)S(1)}, u32[]{:S(2)}, u32[]{:S(2)}) collective-permute-start(f32[3072]{0:T(1024)S(1)} %pad_maximum_fusion.11), channel_id=1, source_target_pairs={{0,3},{1,2},{2,1},{3,0},{4,7},{5,6},{6,5},{7,4},{8,11},{9,10},{10,... | collective-permute-start | bytes 36872 | tf_op jit(solution)/shard_map/ppermute | solution.py:29
  36.3 4.6 %collective-permute-start.12 = (f32[3072]{0:T(1024)S(1)}, f32[3072]{0:T(1024)S(1)}, u32[]{:S(2)}, u32[]{:S(2)}) collective-permute-start(f32[3072]{0:T(1024)S(1)} %pad_maximum_fusion.12), channel_id=1, source_target_pairs={{0,2},{1,3},{2,0},{3,1},{4,6},{5,7},{6,4},{7,5},{8,10},{9,11},{10,... | collective-permute-start | bytes 36872 | tf_op jit(solution)/shard_map/ppermute | solution.py:29
  36.3 4.6 %collective-permute-start.13 = (f32[3072]{0:T(1024)S(1)}, f32[3072]{0:T(1024)S(1)}, u32[]{:S(2)}, u32[]{:S(2)}) collective-permute-start(f32[3072]{0:T(1024)S(1)} %pad_maximum_fusion.13), channel_id=1, source_target_pairs={{0,1},{1,0},{2,3},{3,2},{4,5},{5,4},{6,7},{7,6},{8,9},{9,8},{10,11... | collective-permute-start | bytes 36872 | tf_op jit(solution)/shard_map/ppermute | solution.py:29
